TPU v7x, 512 devices: a whole 4x4x16 slice. The times are simulated.
512 devices in a mesh: sub: 16 (over z), leaf: 32 (over y, x, core).
Axes of the slice: x: 4, y: 4, z: 16, core: 2. Of those that a mesh axis runs over, the one named last changes fastest.
Arguments:
- shift: float32 [1], replicated, may hold values from 0.5 to 2
- self_terms: float32 [524288], P(('leaf', 'sub')), may hold values from 1 to 2
- order: int32 [512, 1024], P(('leaf', 'sub')), may hold values from 0 to 1023, each once within a row
- split: int32 [512], P(('leaf', 'sub')), may hold values from 256 to 768
- coupling: bfloat16 [524288, 768], P(('leaf', 'sub')), as said below
- higher: bfloat16 [524288, 512], P(('leaf', 'sub'))
Outputs:
- applied_higher: bfloat16 [524288, 512], P(('leaf', 'sub'))
Inputs may be any that keep to these rules, and one draw needn't show every extreme that they name: `coupling`: at every node of every level, the symmetric matrix made of diag and the blocks U V^T and V U^T of this and lower levels is positive definite.
All inputs are finite; a program needn't handle non-finite values.
Results may differ from a plain program's by a relative error of at most 0.001.
The roundings to bfloat16 on the way count: a program that leaves them out, or rounds other values in their place, can miss the bound.
Values sent between devices are 32-bit elements; how exact they have to be, the bound alone decides.
A program may use at most 64 MiB of HBM per device.

v0:
```python
import jax
import jax.numpy as jnp
from jax import lax
from jax.sharding import PartitionSpec as P

RANK = 128


def from_partner(value, axis, stride):
    mask = 2**stride
    pairs = [(source, source ^ mask) for source in range(lax.axis_size(axis))]
    return lax.ppermute(value, axis, pairs)


def factor_solve(factor, target):
    lower_part = lax.linalg.triangular_solve(factor, target, left_side=True, lower=True)
    return lax.linalg.triangular_solve(
        factor, lower_part, left_side=True, lower=True, transpose_a=True
    )


def core_terms(left_sum, right_sum):
    width = left_sum.shape[0]
    first = left_sum[:, :width]
    projected = left_sum[:, width:]
    second = right_sum[:, :width]
    beyond = right_sum[:, width:]
    identity_block = jnp.eye(width, dtype=jnp.float32)
    first_factor = jnp.linalg.cholesky(first)
    first_inverse = factor_solve(first_factor, identity_block)
    schur_factor = jnp.linalg.cholesky(first_inverse - second)
    target = beyond - jnp.dot(second, projected, precision=lax.Precision.HIGHEST)
    back = factor_solve(schur_factor, target) - projected
    across = beyond + jnp.dot(second, back, precision=lax.Precision.HIGHEST)
    return (across, back)


def project_rows(basis, columns):
    return lax.dot_general(
        basis, columns, (((0,), (0,)), ((), ())), preferred_element_type=jnp.float32
    )


def node_step(columns, mine, other, is_left):
    left_sum = jnp.where(is_left, mine, other)
    right_sum = jnp.where(is_left, other, mine)
    across, back = core_terms(left_sum, right_sum)
    coefficient = jnp.where(is_left, -across, back).astype(jnp.bfloat16)
    update = columns[:, RANK:].astype(jnp.float32) + jnp.dot(
        columns[:, :RANK], coefficient, preferred_element_type=jnp.float32
    )
    return update.astype(jnp.bfloat16)


def per_device(shift, self_terms, order, split, coupling, higher):
    sub_bits = lax.axis_size("sub").bit_length() - 1
    diagonal = shift[0] + self_terms
    joined = jnp.concatenate([coupling, higher], axis=1).astype(jnp.float32)
    columns = (joined / diagonal[:, None]).astype(jnp.bfloat16)
    inside = (order[0] < split[0]).astype(jnp.bfloat16)[:, None]
    outside = 1 - inside
    basis = coupling[:, :RANK]
    left_sum = project_rows(basis * inside, columns)
    right_sum = project_rows(basis * outside, columns)
    across, back = core_terms(left_sum, right_sum)
    own = columns[:, :RANK]
    update = columns[:, RANK:].astype(jnp.float32)
    update = update + jnp.dot(
        own * inside, (-across).astype(jnp.bfloat16), preferred_element_type=jnp.float32
    )
    update = update + jnp.dot(
        own * outside, back.astype(jnp.bfloat16), preferred_element_type=jnp.float32
    )
    columns = update.astype(jnp.bfloat16)
    position = lax.axis_index("sub")
    for level in range(1, sub_bits + 1):
        basis = coupling[:, level * RANK : (level + 1) * RANK]
        partial_value = project_rows(basis, columns)
        stride = 2 ** (level - 1)
        mine = partial_value
        for bit in range(level - 1):
            mine = mine + from_partner(mine, "sub", bit)
        other = from_partner(mine, "sub", level - 1)
        is_left = position // stride % 2 == 0
        columns = node_step(columns, mine, other, is_left)
    top = sub_bits + 1
    basis = coupling[:, top * RANK : (top + 1) * RANK]
    partial_value = project_rows(basis, columns)
    mine = lax.psum(partial_value, "sub")
    other = from_partner(mine, "leaf", 0)
    is_left = lax.axis_index("leaf") % 2 == 0
    return node_step(columns, mine, other, is_left)


def solution(mesh):
    in_specs = (
        P(),
        P(("leaf", "sub")),
        P(("leaf", "sub"), None),
        P(("leaf", "sub")),
        P(("leaf", "sub"), None),
        P(("leaf", "sub"), None),
    )
    out_specs = P(("leaf", "sub"), None)
    return jax.shard_map(
        per_device, mesh=mesh, in_specs=in_specs, out_specs=out_specs, check_vma=False
    )
```

profile of v0, /device:TPU:1, one launch (start us, length us, event | category | flops | bytes accessed | tf_op | source)
XLA Modules:
  0.0 782.3 jit_solution(3534729396626597273)
XLA Ops:
  9.2 2.3 divide_convert_fusion
  17.2 11.7 %cholesky.194 = f32[128,128]{1,0:T(8,128)S(1)} custom-call(f32[128,128]{1,0:T(8,128)S(1)} %fusion.114), custom_call_target="Cholesky" | custom-call | tf_op jit(solution)/shard_map/jit(cholesky)/cholesky | solution.py:29
  30.1 9.8 %custom-call.55 = f32[1,128,128]{1,2,0:T(8,128)S(1)} custom-call(f32[1,128,128]{2,1,0:T(8,128)S(1)} %fusion.61), custom_call_target="InvertDiagBlocksLowerTriangular" | custom-call | tf_op jit(solution)/shard_map/triangular_solve/custom-call.2 | solution.py:17
  42.2 11.7 %cholesky.205 = f32[128,128]{1,0:T(8,128)S(1)} custom-call(f32[128,128]{1,0:T(8,128)S(1)} %fusion.111), custom_call_target="Cholesky" | custom-call | tf_op jit(solution)/shard_map/jit(cholesky)/cholesky | solution.py:31
  55.4 9.8 %custom-call.38 = f32[1,128,128]{1,2,0:T(8,128)S(1)} custom-call(f32[1,128,128]{2,1,0:T(8,128)S(1)} %fusion.62), custom_call_target="InvertDiagBlocksLowerTriangular" | custom-call | tf_op jit(solution)/shard_map/triangular_solve | solution.py:17
  73.0 4.4 collective-permute-start
  77.4 8.5 %collective-permute-done = f32[128,1152]{0,1:T(8,128)S(1)} collective-permute-done((f32[128,1152]{0,1:T(8,128)S(1)}, f32[128,1152]{0,1:T(8,128)S(1)}, u32[]{:S(2)}, u32[]{:S(2)}) %collective-permute-start) | collective-permute-done | bytes 589856 | tf_op jit(solution)/shard_map/ppermute | solution.py:12
  86.1 11.7 %cholesky.216 = f32[128,128]{1,0:T(8,128)S(1)} custom-call(f32[128,128]{1,0:T(8,128)S(1)} %fusion.107), custom_call_target="Cholesky" | custom-call | tf_op jit(solution)/shard_map/jit(cholesky)/cholesky | solution.py:29
  99.2 9.8 %custom-call.57 = f32[1,128,128]{1,2,0:T(8,128)S(1)} custom-call(f32[1,128,128]{2,1,0:T(8,128)S(1)} %fusion.63), custom_call_target="InvertDiagBlocksLowerTriangular" | custom-call | tf_op jit(solution)/shard_map/triangular_solve/custom-call.2 | solution.py:17
  110.3 11.7 %cholesky.227 = f32[128,128]{1,0:T(8,128)S(1)} custom-call(f32[128,128]{1,0:T(8,128)S(1)} %fusion.104), custom_call_target="Cholesky" | custom-call | tf_op jit(solution)/shard_map/jit(cholesky)/cholesky | solution.py:31
  123.3 21.7 %custom-call.39 = f32[1,128,128]{1,2,0:T(8,128)S(1)} custom-call(f32[1,128,128]{2,1,0:T(8,128)S(1)} %fusion.64), custom_call_target="InvertDiagBlocksLowerTriangular" | custom-call | tf_op jit(solution)/shard_map/triangular_solve | solution.py:17
  147.3 2.4 add_convert_fusion
  151.0 4.1 collective-permute-start.1
  155.1 7.0 collective-permute-done.1
  162.2 12.1 %collective-permute-start.2 = (f32[128,1024]{0,1:T(8,128)S(1)}, f32[128,1024]{0,1:T(8,128)}, u32[]{:S(2)}, u32[]{:S(2)}) collective-permute-start(f32[128,1024]{0,1:T(8,128)S(1)} %add.127), channel_id=1, source_target_pairs={{0,64},{32,96},{64,0},{96,32},{128,192},{160,224},{192,128},{224,1... | collective-permute-start | bytes 1572872 | tf_op jit(solution)/shard_map/ppermute | solution.py:12
  174.4 22.8 %collective-permute-done.2 = f32[128,1024]{0,1:T(8,128)} collective-permute-done((f32[128,1024]{0,1:T(8,128)S(1)}, f32[128,1024]{0,1:T(8,128)}, u32[]{:S(2)}, u32[]{:S(2)}) %collective-permute-start.2) | collective-permute-done | bytes 524320 | tf_op jit(solution)/shard_map/ppermute | solution.py:12
  198.5 11.7 %cholesky.238 = f32[128,128]{1,0:T(8,128)S(1)} custom-call(f32[128,128]{1,0:T(8,128)S(1)} %fusion.100), custom_call_target="Cholesky" | custom-call | tf_op jit(solution)/shard_map/jit(cholesky)/cholesky | solution.py:29
  211.6 9.8 %custom-call.59 = f32[1,128,128]{1,2,0:T(8,128)S(1)} custom-call(f32[1,128,128]{2,1,0:T(8,128)S(1)} %fusion.65), custom_call_target="InvertDiagBlocksLowerTriangular" | custom-call | tf_op jit(solution)/shard_map/triangular_solve/custom-call.2 | solution.py:17
  222.6 11.7 %cholesky.249 = f32[128,128]{1,0:T(8,128)S(1)} custom-call(f32[128,128]{1,0:T(8,128)S(1)} %fusion.97), custom_call_target="Cholesky" | custom-call | tf_op jit(solution)/shard_map/jit(cholesky)/cholesky | solution.py:31
  235.7 10.2 %custom-call.40 = f32[1,128,128]{1,2,0:T(8,128)S(1)} custom-call(f32[1,128,128]{2,1,0:T(8,128)S(1)} %fusion.66), custom_call_target="InvertDiagBlocksLowerTriangular" | custom-call | tf_op jit(solution)/shard_map/triangular_solve | solution.py:17
  247.9 2.2 add_convert_fusion.1
  250.9 2.9 collective-permute-start.3
  253.8 9.7 %collective-permute-done.3 = f32[128,896]{0,1:T(8,128)S(1)} collective-permute-done((f32[128,896]{0,1:T(8,128)S(1)}, f32[128,896]{0,1:T(8,128)S(1)}, u32[]{:S(2)}, u32[]{:S(2)}) %collective-permute-start.3) | collective-permute-done | bytes 458784 | tf_op jit(solution)/shard_map/ppermute | solution.py:12
  263.6 5.7 collective-permute-start.4
  269.3 19.9 %collective-permute-done.4 = f32[128,896]{0,1:T(8,128)S(1)} collective-permute-done((f32[128,896]{0,1:T(8,128)S(1)}, f32[128,896]{0,1:T(8,128)S(1)}, u32[]{:S(2)}, u32[]{:S(2)}) %collective-permute-start.4) | collective-permute-done | bytes 458784 | tf_op jit(solution)/shard_map/ppermute | solution.py:12
  289.3 8.8 %collective-permute-start.5 = (f32[128,896]{0,1:T(8,128)S(1)}, f32[128,896]{0,1:T(8,128)S(1)}, u32[]{:S(2)}, u32[]{:S(2)}) collective-permute-start(f32[128,896]{0,1:T(8,128)S(1)} %add.132), channel_id=1, source_target_pairs={{0,128},{32,160},{64,192},{96,224},{128,0},{160,32},{192,64},{224,... | collective-permute-start | bytes 1376264 | tf_op jit(solution)/shard_map/ppermute | solution.py:12
  298.1 39.4 %collective-permute-done.5 = f32[128,896]{0,1:T(8,128)S(1)} collective-permute-done((f32[128,896]{0,1:T(8,128)S(1)}, f32[128,896]{0,1:T(8,128)S(1)}, u32[]{:S(2)}, u32[]{:S(2)}) %collective-permute-start.5) | collective-permute-done | bytes 458784 | tf_op jit(solution)/shard_map/ppermute | solution.py:12
  337.7 11.7 %cholesky.260 = f32[128,128]{1,0:T(8,128)S(1)} custom-call(f32[128,128]{1,0:T(8,128)S(1)} %fusion.93), custom_call_target="Cholesky" | custom-call | tf_op jit(solution)/shard_map/jit(cholesky)/cholesky | solution.py:29
  350.7 9.8 %custom-call.61 = f32[1,128,128]{1,2,0:T(8,128)S(1)} custom-call(f32[1,128,128]{2,1,0:T(8,128)S(1)} %fusion.67), custom_call_target="InvertDiagBlocksLowerTriangular" | custom-call | tf_op jit(solution)/shard_map/triangular_solve/custom-call.2 | solution.py:17
  361.7 11.7 %cholesky.271 = f32[128,128]{1,0:T(8,128)S(1)} custom-call(f32[128,128]{1,0:T(8,128)S(1)} %fusion.90), custom_call_target="Cholesky" | custom-call | tf_op jit(solution)/shard_map/jit(cholesky)/cholesky | solution.py:31
  374.8 9.9 %custom-call.41 = f32[1,128,128]{1,2,0:T(8,128)S(1)} custom-call(f32[1,128,128]{2,1,0:T(8,128)S(1)} %fusion.68), custom_call_target="InvertDiagBlocksLowerTriangular" | custom-call | tf_op jit(solution)/shard_map/triangular_solve | solution.py:17
  391.2 10.1 %collective-permute-done.6 = f32[128,768]{0,1:T(8,128)S(1)} collective-permute-done((f32[128,768]{0,1:T(8,128)S(1)}, f32[128,768]{0,1:T(8,128)S(1)}, u32[]{:S(2)}, u32[]{:S(2)}) %collective-permute-start.6) | collective-permute-done | bytes 393248 | tf_op jit(solution)/shard_map/ppermute | solution.py:12
  403.3 20.3 %collective-permute-done.7 = f32[128,768]{0,1:T(8,128)S(1)} collective-permute-done((f32[128,768]{0,1:T(8,128)S(1)}, f32[128,768]{0,1:T(8,128)S(1)}, u32[]{:S(2)}, u32[]{:S(2)}) %collective-permute-start.7) | collective-permute-done | bytes 393248 | tf_op jit(solution)/shard_map/ppermute | solution.py:12
  423.7 4.3 collective-permute-start.8
  428.0 35.9 %collective-permute-done.8 = f32[128,768]{0,1:T(8,128)S(1)} collective-permute-done((f32[128,768]{0,1:T(8,128)S(1)}, f32[128,768]{0,1:T(8,128)S(1)}, u32[]{:S(2)}, u32[]{:S(2)}) %collective-permute-start.8) | collective-permute-done | bytes 393248 | tf_op jit(solution)/shard_map/ppermute | solution.py:12
  464.7 19.0 %collective-permute-start.9 = (f32[128,768]{0,1:T(8,128)}, f32[128,768]{0,1:T(8,128)}, u32[]{:S(2)}, u32[]{:S(2)}) collective-permute-start(f32[128,768]{0,1:T(8,128)} %add.138), channel_id=1, source_target_pairs={{0,256},{32,288},{64,320},{96,352},{128,384},{160,416},{192,448},{... | collective-permute-start | bytes 1179656 | tf_op jit(solution)/shard_map/ppermute | solution.py:12
  483.7 14.6 %collective-permute-done.9 = f32[128,768]{0,1:T(8,128)} collective-permute-done((f32[128,768]{0,1:T(8,128)}, f32[128,768]{0,1:T(8,128)}, u32[]{:S(2)}, u32[]{:S(2)}) %collective-permute-start.9) | collective-permute-done | bytes 393248 | tf_op jit(solution)/shard_map/ppermute | solution.py:12
  503.9 13.2 %cholesky.282 = f32[128,128]{1,0:T(8,128)} custom-call(f32[128,128]{1,0:T(8,128)} %fusion.86), custom_call_target="Cholesky" | custom-call | tf_op jit(solution)/shard_map/jit(cholesky)/cholesky | solution.py:29
  520.7 11.3 %custom-call.63 = f32[1,128,128]{1,2,0:T(8,128)} custom-call(f32[1,128,128]{2,1,0:T(8,128)} %fusion.69), custom_call_target="InvertDiagBlocksLowerTriangular" | custom-call | tf_op jit(solution)/shard_map/triangular_solve/custom-call.2 | solution.py:17
  540.1 13.2 %cholesky.293 = f32[128,128]{1,0:T(8,128)} custom-call(f32[128,128]{1,0:T(8,128)} %fusion.83), custom_call_target="Cholesky" | custom-call | tf_op jit(solution)/shard_map/jit(cholesky)/cholesky | solution.py:31
  556.9 11.4 %custom-call.42 = f32[1,128,128]{1,2,0:T(8,128)} custom-call(f32[1,128,128]{2,1,0:T(8,128)} %fusion.70), custom_call_target="InvertDiagBlocksLowerTriangular" | custom-call | tf_op jit(solution)/shard_map/triangular_solve | solution.py:17
  575.8 133.2 %all-reduce.2.cloned.1.call-done = f32[128,640]{0,1:T(8,128)} async-done(((f32[128,640]{0,1:T(8,128)}), f32[128,640]{0,1:T(8,128)}) %all-reduce.2.cloned.1.call-update) | async-done | bytes 327696 | tf_op jit(solution)/shard_map/psum | solution.py:89
  708.9 12.3 %collective-permute-start.10 = (f32[128,640]{0,1:T(8,128)}, f32[128,640]{0,1:T(8,128)S(1)}, u32[]{:S(2)}, u32[]{:S(2)}) collective-permute-start(f32[128,640]{0,1:T(8,128)} %all-reduce.2.cloned.1.call-done), channel_id=1, source_target_pairs={{0,1},{1,0},{2,3},{3,2},{4,5},{5,4},{6,7},{7,6},{8,9},{9,8},{10,11... | collective-permute-start | bytes 983048 | tf_op jit(solution)/shard_map/ppermute | solution.py:12
  723.9 11.7 %cholesky.304 = f32[128,128]{1,0:T(8,128)S(1)} custom-call(f32[128,128]{1,0:T(8,128)S(1)} %fusion.79), custom_call_target="Cholesky" | custom-call | tf_op jit(solution)/shard_map/jit(cholesky)/cholesky | solution.py:29
  736.9 9.8 %custom-call.65 = f32[1,128,128]{1,2,0:T(8,128)S(1)} custom-call(f32[1,128,128]{2,1,0:T(8,128)S(1)} %fusion.71), custom_call_target="InvertDiagBlocksLowerTriangular" | custom-call | tf_op jit(solution)/shard_map/triangular_solve/custom-call.2 | solution.py:17
  747.8 11.7 %cholesky.315 = f32[128,128]{1,0:T(8,128)S(1)} custom-call(f32[128,128]{1,0:T(8,128)S(1)} %fusion.76), custom_call_target="Cholesky" | custom-call | tf_op jit(solution)/shard_map/jit(cholesky)/cholesky | solution.py:31
  760.9 10.0 %custom-call.43 = f32[1,128,128]{1,2,0:T(8,128)S(1)} custom-call(f32[1,128,128]{2,1,0:T(8,128)S(1)} %fusion.72), custom_call_target="InvertDiagBlocksLowerTriangular" | custom-call | tf_op jit(solution)/shard_map/triangular_solve | solution.py:17
  772.3 2.7 add_convert_fusion.4
  (146 shorter events, 84.4 us)
Async XLA Ops:
  6.5 702.4 %all-reduce.2.cloned.1.call-start = ((), (), s32[]{:S(2)}) async-start(), calls=%async_computation | async-start | bytes 655360 | tf_op jit(solution)/shard_map/psum | solution.py:89
  14.8 0.8 copy-start.5
  71.0 2.0 copy-start
  73.0 12.9 %collective-permute-start = (f32[128,1152]{0,1:T(8,128)S(1)}, f32[128,1152]{0,1:T(8,128)S(1)}, u32[]{:S(2)}, u32[]{:S(2)}) collective-permute-start(f32[128,1152]{0,1:T(8,128)S(1)} %convolution_bitcast_fusion), channel_id=1, source_target_pairs={{0,32},{32,0},{64,96},{96,64},{128,160},{160,128},{192,224},{224,1... | collective-permute-start | bytes 1769480 | tf_op jit(solution)/shard_map/ppermute | solution.py:12
  146.7 3.0 copy-start.1
  149.7 1.4 copy-start.2
  151.0 11.1 %collective-permute-start.1 = (f32[128,1024]{0,1:T(8,128)S(1)}, f32[128,1024]{0,1:T(8,128)S(1)}, u32[]{:S(2)}, u32[]{:S(2)}) collective-permute-start(f32[128,1024]{0,1:T(8,128)S(1)} %convolution_bitcast_fusion.1), channel_id=1, source_target_pairs={{0,32},{32,0},{64,96},{96,64},{128,160},{160,128},{192,224},{224,1... | collective-permute-start | bytes 1572872 | tf_op jit(solution)/shard_map/ppermute | solution.py:12
  162.2 35.0 %collective-permute-start.2 = (f32[128,1024]{0,1:T(8,128)S(1)}, f32[128,1024]{0,1:T(8,128)}, u32[]{:S(2)}, u32[]{:S(2)}) collective-permute-start(f32[128,1024]{0,1:T(8,128)S(1)} %add.127), channel_id=1, source_target_pairs={{0,64},{32,96},{64,0},{96,32},{128,192},{160,224},{192,128},{224,1... | collective-permute-start | bytes 1572872 | tf_op jit(solution)/shard_map/ppermute | solution.py:12
  250.2 39.1 %copy-start.3 = (bf16[1024,896]{1,0:T(8,128)(2,1)}, bf16[1024,896]{1,0:T(8,128)(2,1)S(1)}, u32[]{:S(2)}) copy-start(bf16[1024,896]{1,0:T(8,128)(2,1)S(1)} %add_convert_fusion.1) | copy-start | bytes 5505028
  250.9 12.7 %collective-permute-start.3 = (f32[128,896]{0,1:T(8,128)S(1)}, f32[128,896]{0,1:T(8,128)S(1)}, u32[]{:S(2)}, u32[]{:S(2)}) collective-permute-start(f32[128,896]{0,1:T(8,128)S(1)} %convolution_bitcast_fusion.2), channel_id=1, source_target_pairs={{0,32},{32,0},{64,96},{96,64},{128,160},{160,128},{192,224},{224,1... | collective-permute-start | bytes 1376264 | tf_op jit(solution)/shard_map/ppermute | solution.py:12
  263.6 25.6 %collective-permute-start.4 = (f32[128,896]{0,1:T(8,128)S(1)}, f32[128,896]{0,1:T(8,128)S(1)}, u32[]{:S(2)}, u32[]{:S(2)}) collective-permute-start(f32[128,896]{0,1:T(8,128)S(1)} %add.131), channel_id=1, source_target_pairs={{0,64},{32,96},{64,0},{96,32},{128,192},{160,224},{192,128},{224,1... | collective-permute-start | bytes 1376264 | tf_op jit(solution)/shard_map/ppermute | solution.py:12
  289.3 48.2 %collective-permute-start.5 = (f32[128,896]{0,1:T(8,128)S(1)}, f32[128,896]{0,1:T(8,128)S(1)}, u32[]{:S(2)}, u32[]{:S(2)}) collective-permute-start(f32[128,896]{0,1:T(8,128)S(1)} %add.132), channel_id=1, source_target_pairs={{0,128},{32,160},{64,192},{96,224},{128,0},{160,32},{192,64},{224,... | collective-permute-start | bytes 1376264 | tf_op jit(solution)/shard_map/ppermute | solution.py:12
  389.2 12.1 %collective-permute-start.6 = (f32[128,768]{0,1:T(8,128)S(1)}, f32[128,768]{0,1:T(8,128)S(1)}, u32[]{:S(2)}, u32[]{:S(2)}) collective-permute-start(f32[128,768]{0,1:T(8,128)S(1)} %convolution_bitcast_fusion.3), channel_id=1, source_target_pairs={{0,32},{32,0},{64,96},{96,64},{128,160},{160,128},{192,224},{224,1... | collective-permute-start | bytes 1179656 | tf_op jit(solution)/shard_map/ppermute | solution.py:12
  401.4 22.2 %collective-permute-start.7 = (f32[128,768]{0,1:T(8,128)S(1)}, f32[128,768]{0,1:T(8,128)S(1)}, u32[]{:S(2)}, u32[]{:S(2)}) collective-permute-start(f32[128,768]{0,1:T(8,128)S(1)} %add.136), channel_id=1, source_target_pairs={{0,64},{32,96},{64,0},{96,32},{128,192},{160,224},{192,128},{224,1... | collective-permute-start | bytes 1179656 | tf_op jit(solution)/shard_map/ppermute | solution.py:12
  423.7 40.2 %collective-permute-start.8 = (f32[128,768]{0,1:T(8,128)S(1)}, f32[128,768]{0,1:T(8,128)S(1)}, u32[]{:S(2)}, u32[]{:S(2)}) collective-permute-start(f32[128,768]{0,1:T(8,128)S(1)} %add.137), channel_id=1, source_target_pairs={{0,128},{32,160},{64,192},{96,224},{128,0},{160,32},{192,64},{224,... | collective-permute-start | bytes 1179656 | tf_op jit(solution)/shard_map/ppermute | solution.py:12
  464.7 33.7 %collective-permute-start.9 = (f32[128,768]{0,1:T(8,128)}, f32[128,768]{0,1:T(8,128)}, u32[]{:S(2)}, u32[]{:S(2)}) collective-permute-start(f32[128,768]{0,1:T(8,128)} %add.138), channel_id=1, source_target_pairs={{0,256},{32,288},{64,320},{96,352},{128,384},{160,416},{192,448},{... | collective-permute-start | bytes 1179656 | tf_op jit(solution)/shard_map/ppermute | solution.py:12
  573.4 1.1 copy-start.4
  708.9 13.8 %collective-permute-start.10 = (f32[128,640]{0,1:T(8,128)}, f32[128,640]{0,1:T(8,128)S(1)}, u32[]{:S(2)}, u32[]{:S(2)}) collective-permute-start(f32[128,640]{0,1:T(8,128)} %all-reduce.2.cloned.1.call-done), channel_id=1, source_target_pairs={{0,1},{1,0},{2,3},{3,2},{4,5},{5,4},{6,7},{7,6},{8,9},{9,8},{10,11... | collective-permute-start | bytes 983048 | tf_op jit(solution)/shard_map/ppermute | solution.py:12
Sparse Core Ops, SparseCore 0:
  575.9 133.0 all-reduce.1
where the time goes:
time: 793 us; the launch traced here: 782 us
  waiting for transfers between devices  323 us (41%)
  other arithmetic  310 us (39%)
  starting transfers between devices  77.5 us (10%)
  matrix products  48.2 us (6%)
  between operations  16.1 us (2%)
    ppermute x11, waiting for transfers between devices, from_partner(): return lax.ppermute(value, axis, pairs)  190 us
    another operation x24, other arithmetic, factor_solve(): lax.linalg.triangular_solve(factor, lower_part, left_side=True, lower=Tru...  144 us
    psum x1, waiting for transfers between devices, per_device(): mine = lax.psum(partial_value, 'sub')  133 us
    ppermute x11, starting transfers between devices, from_partner(): return lax.ppermute(value, axis, pairs)  77.5 us
    another operation x18, other arithmetic, core_terms(): schur_factor = jnp.linalg.cholesky(first_inverse - second)  76.9 us
    another operation x18, other arithmetic, core_terms(): first_factor = jnp.linalg.cholesky(first)  76.6 us
  transfers between devices with their start and end apart: 12, of which 12 were waited for; matrix products, arithmetic and copies ran while one was open for 0% of the time, Pallas kernels for 0%

commit v1 on v0

v1 whole, which is shorter than its diff:
```python
import functools
import jax
import jax.numpy as jnp
from jax import lax
from jax.experimental import pallas as pl
from jax.experimental.pallas import tpu as pltpu
from jax.sharding import PartitionSpec as P

RANK = 128
CHUNK_ROWS = 64
PACE = 3
HIGHEST = lax.Precision.HIGHEST
VMEM = pltpu.VMEM


def dot32(a, b):
    return jnp.dot(a, b, precision=HIGHEST, preferred_element_type=jnp.float32)


def dot16(a, b):
    return jnp.dot(a, b, preferred_element_type=jnp.float32)


def identity():
    shape = (RANK, RANK)
    rows = lax.broadcasted_iota(jnp.int32, shape, 0)
    cols = lax.broadcasted_iota(jnp.int32, shape, 1)
    return jnp.where(rows == cols, 1.0, 0.0).astype(jnp.float32)


def symmetric(value):
    return 0.5 * (value + value.T)


def invert(other, mine, inv_ref, pow_ref):
    step = dot32(other, mine)
    inv_ref[...] = identity() + step
    power = dot32(step, step)
    pow_ref[...] = power

    def unfinished(carry):
        count, size = carry
        return (count < 48) & (size > 1e-16)

    def more(carry):
        count, _ = carry
        inverse = inv_ref[...]
        power = pow_ref[...]
        inv_ref[...] = inverse + dot32(inverse, power)
        power = dot32(power, power)
        pow_ref[...] = power
        return count + 1, jnp.sum(power * power)

    lax.while_loop(unfinished, more, (jnp.int32(0), jnp.sum(power * power)))


def column_blocks(count, body):
    pairs = count // 2

    @pl.loop(0, pairs)
    def _(pair):
        body(2 * pair, 2)

    if count % 2:
        body(count - 1, 1)


def lanes(start, width):
    first = start * RANK
    if not isinstance(first, int):
        first = pl.multiple_of(first, RANK)
    return pl.ds(first, width * RANK)


def side_by_side(ref, first, width):
    return jnp.concatenate([ref[first + i] for i in range(width)], axis=1)


def update_blocks(columns_ref, left_ref, coefs_of, next_ref, out_ref, partial_ref):
    count = out_ref.shape[1] // RANK

    def body(first, width):
        coef = coefs_of(first, width).astype(jnp.bfloat16)
        rest = columns_ref[:, lanes(first + 1, width)].astype(jnp.float32)
        fresh = (rest + dot16(left_ref[...], coef)).astype(jnp.bfloat16)
        out_ref[:, lanes(first, width)] = fresh
        if partial_ref is not None:
            sums = dot16(next_ref[...], fresh)
            for i in range(width):
                partial_ref[first + i] = sums[:, i * RANK : (i + 1) * RANK]

    column_blocks(count, body)


def start_kernel(
    shift_ref, split_ref, terms_ref, order_ref, coupling_ref, higher_ref,
    out_ref, partial_ref,
    columns_ref, own_ref, basis_t_ref, next_ref, sums_ref, mix_ref, inv_ref, pow_ref,
):
    rows = coupling_ref.shape[0]
    levels = coupling_ref.shape[1]
    shift = shift_ref[0]
    split = split_ref[0]
    for block in range(rows // RANK):
        here = pl.ds(block * RANK, RANK)
        diagonal = shift + terms_ref[pl.ds(block, 1), :]
        scale = jnp.broadcast_to(1.0 / diagonal, (RANK, RANK)).T
        mask = jnp.where(order_ref[pl.ds(block, 1), :] < split, 1.0, 0.0)
        inside_t = jnp.broadcast_to(mask, (RANK, RANK))
        inside = inside_t.T
        for first in range(0, levels, RANK):
            value = coupling_ref[here, pl.ds(first, RANK)].astype(jnp.float32)
            columns_ref[here, pl.ds(first, RANK)] = (value * scale).astype(jnp.bfloat16)
        for first in range(0, higher_ref.shape[1], RANK):
            value = higher_ref[here, pl.ds(first, RANK)].astype(jnp.float32)
            columns_ref[here, pl.ds(levels + first, RANK)] = (value * scale).astype(jnp.bfloat16)
        own = columns_ref[here, pl.ds(0, RANK)].astype(jnp.float32)
        own_ref[here, pl.ds(0, RANK)] = (own * inside).astype(jnp.bfloat16)
        own_ref[here, pl.ds(RANK, RANK)] = (own * (1.0 - inside)).astype(jnp.bfloat16)
        basis_t = coupling_ref[here, pl.ds(0, RANK)].astype(jnp.float32).T
        basis_t_ref[pl.ds(0, RANK), here] = (basis_t * inside_t).astype(jnp.bfloat16)
        basis_t_ref[pl.ds(RANK, RANK), here] = (basis_t * (1.0 - inside_t)).astype(jnp.bfloat16)
        later = coupling_ref[here, pl.ds(RANK, RANK)].astype(jnp.float32)
        next_ref[:, here] = later.T.astype(jnp.bfloat16)

    def project(first, width):
        sums_ref[:, lanes(first, width)] = dot16(
            basis_t_ref[...], columns_ref[:, lanes(first, width)]
        )

    column_blocks(columns_ref.shape[1] // RANK, project)
    first = symmetric(sums_ref[pl.ds(0, RANK), pl.ds(0, RANK)])
    second = symmetric(sums_ref[pl.ds(RANK, RANK), pl.ds(0, RANK)])
    invert(second, first, inv_ref, pow_ref)
    inverse = inv_ref[...]
    mix_ref[pl.ds(0, RANK), pl.ds(0, RANK)] = dot32(inverse, second)
    mix_ref[pl.ds(0, RANK), pl.ds(RANK, RANK)] = -inverse
    inverse = inverse.T
    mix_ref[pl.ds(RANK, RANK), pl.ds(0, RANK)] = -inverse
    mix_ref[pl.ds(RANK, RANK), pl.ds(RANK, RANK)] = dot32(inverse, first)

    def coefs_of(first, width):
        return dot32(mix_ref[...], sums_ref[:, lanes(first + 1, width)])

    update_blocks(columns_ref, own_ref, coefs_of, next_ref, out_ref, partial_ref)


def level_kernel(last, columns_ref, mine_ref, other_ref, *refs):
    if last:
        out_ref, own_ref, mix_ref, inv_ref, pow_ref = refs
        basis_ref = partial_ref = next_ref = None
    else:
        basis_ref, out_ref, partial_ref, own_ref, mix_ref, inv_ref, pow_ref, next_ref = refs
        for block in range(basis_ref.shape[0] // RANK):
            here = pl.ds(block * RANK, RANK)
            later = basis_ref[here, :].astype(jnp.float32)
            next_ref[:, here] = later.T.astype(jnp.bfloat16)
    own_ref[...] = columns_ref[:, pl.ds(0, RANK)]
    mine = symmetric(mine_ref[0])
    other = symmetric(other_ref[0])
    invert(other, mine, inv_ref, pow_ref)
    inverse = inv_ref[...]
    mix_ref[:, pl.ds(0, RANK)] = dot32(inverse, other)
    mix_ref[:, pl.ds(RANK, RANK)] = -inverse

    def coefs_of(first, width):
        sums = jnp.concatenate(
            [side_by_side(mine_ref, first + 1, width), side_by_side(other_ref, first + 1, width)],
            axis=0,
        )
        return dot32(mix_ref[...], sums)

    update_blocks(columns_ref, own_ref, coefs_of, next_ref, out_ref, partial_ref)


def start_call(shift, split, terms, order, coupling, higher):
    rows, levels = coupling.shape
    width = levels + higher.shape[1]
    rest = width - RANK
    whole = pl.BlockSpec(memory_space=VMEM)
    scalar = pl.BlockSpec(memory_space=pltpu.SMEM)
    return pl.pallas_call(
        start_kernel,
        name="start",
        out_shape=(
            jax.ShapeDtypeStruct((rows, rest), jnp.bfloat16),
            jax.ShapeDtypeStruct((rest // RANK, RANK, RANK), jnp.float32),
        ),
        in_specs=[scalar, scalar, whole, whole, whole, whole],
        out_specs=(whole, whole),
        scratch_shapes=[
            VMEM((rows, width), jnp.bfloat16),
            VMEM((rows, 2 * RANK), jnp.bfloat16),
            VMEM((2 * RANK, rows), jnp.bfloat16),
            VMEM((RANK, rows), jnp.bfloat16),
            VMEM((2 * RANK, width), jnp.float32),
            VMEM((2 * RANK, 2 * RANK), jnp.float32),
            VMEM((RANK, RANK), jnp.float32),
            VMEM((RANK, RANK), jnp.float32),
        ],
        compiler_params=pltpu.CompilerParams(vmem_limit_bytes=40 * 2**20),
    )(shift, split, terms.reshape(rows // RANK, RANK), order.reshape(rows // RANK, RANK), coupling, higher)


def level_call(level, columns, mine, other, coupling):
    rows, width = columns.shape
    rest = width - RANK
    last = coupling is None
    out_shape = [jax.ShapeDtypeStruct((rows, rest), jnp.bfloat16)]
    scratch = [
        VMEM((rows, RANK), jnp.bfloat16),
        VMEM((RANK, 2 * RANK), jnp.float32),
        VMEM((RANK, RANK), jnp.float32),
        VMEM((RANK, RANK), jnp.float32),
    ]

    def all_of(shape):
        return pl.BlockSpec(shape, lambda i: (0,) * len(shape))

    in_specs = [all_of(columns.shape), all_of(mine.shape), all_of(other.shape)]
    operands = [columns, mine, other]
    if not last:
        out_shape.append(jax.ShapeDtypeStruct((rest // RANK, RANK, RANK), jnp.float32))
        scratch.append(VMEM((RANK, rows), jnp.bfloat16))
        in_specs.append(pl.BlockSpec((rows, RANK), lambda i: (0, level + 1)))
        operands.append(coupling)
    return pl.pallas_call(
        functools.partial(level_kernel, last),
        name=f"level{level}",
        grid=(1,),
        out_shape=out_shape,
        in_specs=in_specs,
        out_specs=[all_of(shape.shape) for shape in out_shape],
        scratch_shapes=scratch,
        compiler_params=pltpu.CompilerParams(vmem_limit_bytes=40 * 2**20),
    )(*operands)


def share_kernel(
    span, kind, part_ref, mine_ref, other_ref,
    before, after, cross, up_buf, down_buf,
    before_sem, after_sem, cross_sem, up_sem, down_sem, pass_sem, swap_sem,
):
    chunks = part_ref.shape[0]
    place = lax.axis_index("sub")
    size = lax.axis_size("sub")
    leaf = lax.axis_index("leaf")
    above = {"sub": lax.rem(place + 1, size)}
    below = {"sub": lax.rem(place + size - 1, size)}
    partner = {"leaf": leaf + 1 - 2 * lax.rem(leaf, 2)}
    spot = lax.rem(place, span)
    first_child = lax.rem(place // span, 2) == 0
    has_below = spot > 0
    has_above = spot < span - 1
    if kind == "line":
        node_spot = lax.rem(place, 2 * span)
        link_below = node_spot > 0
        link_above = node_spot < 2 * span - 1
    elif kind == "core":
        link_below = has_below
        link_above = has_above
    barrier = pltpu.get_barrier_semaphore()
    if kind == "ring":
        pl.semaphore_signal(barrier, inc=1, device_id=below)
        pl.semaphore_signal(barrier, inc=1, device_id=above)
        pl.semaphore_wait(barrier, 2)
    else:

        @pl.when(link_below)
        def _():
            pl.semaphore_signal(barrier, inc=1, device_id=below)

        @pl.when(link_above)
        def _():
            pl.semaphore_signal(barrier, inc=1, device_id=above)

        greeted = link_below.astype(jnp.int32) + link_above.astype(jnp.int32)
        if kind == "core":
            pl.semaphore_signal(barrier, inc=1, device_id=partner)
            greeted = greeted + 1
        pl.semaphore_wait(barrier, greeted)

    def copy(src, dst, send, recv, c, to):
        return pltpu.make_async_remote_copy(
            src_ref=src.at[c], dst_ref=dst.at[c], send_sem=send.at[c], recv_sem=recv.at[c],
            device_id=to, device_id_type=pl.DeviceIdType.MESH,
        )

    def go_up(c):
        return copy(up_buf, before, up_sem, before_sem, c, above)

    def go_down(c):
        return copy(down_buf, after, down_sem, after_sem, c, below)

    def pass_up(c):
        return copy(cross, cross, pass_sem, cross_sem, c, above)

    def pass_down(c):
        return copy(cross, cross, pass_sem, cross_sem, c, below)

    def swap(c, to):
        return copy(mine_ref, cross, swap_sem, cross_sem, c, to)

    if kind == "line":
        distance = jnp.where(first_child, span - spot, spot + 1)
        forward_down = first_child & has_below
        forward_up = jnp.logical_not(first_child) & has_above
        swap_up = first_child & (spot == span - 1)
        swap_down = jnp.logical_not(first_child) & (spot == 0)
        cross_from = PACE * (span - 1 + distance)
    elif kind == "ring":
        half = span // 2
        upper = spot >= half
        distance = jnp.where(upper, span - spot, spot + 1)
        forward_down = upper & (spot > half)
        forward_up = jnp.logical_not(upper) & (spot < half - 1)
        swap_up = spot == span - 1
        swap_down = spot == 0
        cross_from = PACE * (span - 1 + distance)
    else:
        cross_from = PACE * jnp.maximum(spot, span - 1 - spot) + PACE

    up_from = PACE * spot
    down_from = PACE * (span - 1 - spot)
    sum_from = jnp.maximum(up_from, down_from)

    def within(c):
        return (c >= 0) & (c < chunks)

    if kind == "core":
        total_slots = chunks + PACE * (span - 1) + PACE
    elif kind == "ring":
        total_slots = chunks + PACE * (span - 1 + span // 2)
    else:
        total_slots = chunks + PACE * (2 * span - 1)

    @pl.loop(0, total_slots)
    def _(slot):
        if span > 1:
            c = slot - up_from

            @pl.when(within(c))
            def _():
                @pl.when(has_below)
                def _():
                    go_up(c).wait_recv()

                @pl.when(has_above & has_below)
                def _():
                    up_buf[c] = part_ref[c] + before[c]

                @pl.when(has_above & jnp.logical_not(has_below))
                def _():
                    up_buf[c] = part_ref[c]

                @pl.when(has_above)
                def _():
                    go_up(c).start()

            d = slot - down_from

            @pl.when(within(d))
            def _():
                @pl.when(has_above)
                def _():
                    go_down(d).wait_recv()

                @pl.when(has_above & has_below)
                def _():
                    down_buf[d] = part_ref[d] + after[d]

                @pl.when(has_below & jnp.logical_not(has_above))
                def _():
                    down_buf[d] = part_ref[d]

                @pl.when(has_below)
                def _():
                    go_down(d).start()

        e = slot - sum_from

        @pl.when(within(e))
        def _():
            if span == 1:
                mine_ref[e] = part_ref[e]
            else:

                @pl.when(has_above & has_below)
                def _():
                    mine_ref[e] = part_ref[e] + before[e] + after[e]

                @pl.when(has_below & jnp.logical_not(has_above))
                def _():
                    mine_ref[e] = part_ref[e] + before[e]

                @pl.when(has_above & jnp.logical_not(has_below))
                def _():
                    mine_ref[e] = part_ref[e] + after[e]

            if kind == "core":
                swap(e, partner).start()
            else:

                @pl.when(swap_up)
                def _():
                    swap(e, above).start()

                @pl.when(swap_down)
                def _():
                    swap(e, below).start()

        x = slot - cross_from

        @pl.when(within(x))
        def _():
            swap(x, partner).wait_recv()
            if kind != "core":

                @pl.when(forward_up)
                def _():
                    pass_up(x).start()

                @pl.when(forward_down)
                def _():
                    pass_down(x).start()

            other_ref[x] = cross[x]

    @pl.loop(0, chunks)
    def _(c):
        if span > 1:

            @pl.when(has_above)
            def _():
                go_up(c).wait_send()

            @pl.when(has_below)
            def _():
                go_down(c).wait_send()

        if kind == "core":
            swap(c, partner).wait_send()
        else:

            @pl.when(swap_up | swap_down)
            def _():
                swap(c, above).wait_send()

            @pl.when(forward_up | forward_down)
            def _():
                pass_up(c).wait_send()


def share_call(level, span, kind, partial):
    blocks = partial.shape[0]
    split = RANK // CHUNK_ROWS
    chunks = blocks * split
    shape = (chunks, CHUNK_ROWS, RANK)
    whole = pl.BlockSpec(memory_space=VMEM)
    buffer = VMEM(shape, jnp.float32)
    semaphores = pltpu.SemaphoreType.DMA((chunks,))
    mine, other = pl.pallas_call(
        functools.partial(share_kernel, span, kind),
        name=f"share{level}",
        out_shape=(jax.ShapeDtypeStruct(shape, jnp.float32),) * 2,
        in_specs=[whole],
        out_specs=(whole, whole),
        scratch_shapes=[buffer] * 5 + [semaphores] * 7,
        compiler_params=pltpu.CompilerParams(
            collective_id=level, has_side_effects=True, vmem_limit_bytes=24 * 2**20
        ),
    )(partial.reshape(shape))
    full = (blocks, RANK, RANK)
    return mine.reshape(full), other.reshape(full)


def per_device(shift, self_terms, order, split, coupling, higher):
    sub_bits = lax.axis_size("sub").bit_length() - 1
    columns, partial = start_call(shift, split, self_terms, order[0], coupling, higher)
    for level in range(1, sub_bits + 1):
        span = 2 ** (level - 1)
        kind = "ring" if level == sub_bits else "line"
        mine, other = share_call(level, span, kind, partial)
        columns, partial = level_call(level, columns, mine, other, coupling)
    mine, other = share_call(sub_bits + 1, lax.axis_size("sub"), "core", partial)
    (columns,) = level_call(sub_bits + 1, columns, mine, other, None)
    return columns


def solution(mesh):
    in_specs = (
        P(),
        P(("leaf", "sub")),
        P(("leaf", "sub"), None),
        P(("leaf", "sub")),
        P(("leaf", "sub"), None),
        P(("leaf", "sub"), None),
    )
    out_specs = P(("leaf", "sub"), None)
    return jax.shard_map(
        per_device, mesh=mesh, in_specs=in_specs, out_specs=out_specs, check_vma=False
    )
```

time: 793 us -> 229 us (0.29); the launches traced: 782 us -> 229 us
  waiting for transfers between devices: 323 us -> 0 us
  other arithmetic: 310 us -> 0 us
  Pallas kernels: 0 us -> 224 us
  starting transfers between devices: 77.5 us -> 0 us
  matrix products: 48.2 us -> 0 us
  between operations: 16.1 us -> 1.39 us
    another operation x60 -> x0, other arithmetic: 298 us -> none  [the longest x24 144 us: factor_solve(): lax.linalg.triangular_solve(factor, lower_part, left_side=True, lower=Tru...]
    pallas_call x0 -> x11, Pallas kernels: none -> 224 us  [the longest x5 194 us: share_call(): pl.pallas_call(functools.partial(share_kernel, span, kind), name=f'share{...]
    ppermute x11 -> x0, waiting for transfers between devices: 190 us -> none  [from_partner(): return lax.ppermute(value, axis, pairs)]
    psum x1 -> x0, waiting for transfers between devices: 133 us -> none  [per_device(): mine = lax.psum(partial_value, 'sub')]
    ppermute x11 -> x0, starting transfers between devices: 77.5 us -> none  [from_partner(): return lax.ppermute(value, axis, pairs)]
    dot_general x26 -> x0, matrix products: 30.7 us -> none  [the longest x5 9.97 us: node_step(): jnp.dot(columns[:, :RANK], coefficient, preferred_element_type=jnp.float32)]
    another operation x24 -> x0, matrix products: 17.5 us -> none  [the longest x12 9.51 us: factor_solve(): lax.linalg.triangular_solve(factor, lower_part, left_side=True, lower=Tru...]
  transfers between devices with their start and end apart: 12 -> 0, of which waited for: 12 -> 0; matrix products, arithmetic and copies ran while one was open for 0% -> 0% of each run, Pallas kernels for 0% -> 0%
where the time goes in v1:
time: 229 us
  Pallas kernels  224 us (98%)
  local copies, waits for them, and re-layouts  4 us (2%)
    pallas_call x5, Pallas kernels, share_call(): pl.pallas_call(functools.partial(share_kernel, span, kind), name=f'share{...  194 us
    pallas_call x5, Pallas kernels, level_call(): pl.pallas_call(functools.partial(level_kernel, last), name=f'level{level}...  20.8 us
    pallas_call x1, Pallas kernels, start_call(): pl.pallas_call(start_kernel, name='start', out_shape=(jax.ShapeDtypeStruc...  9.31 us

profile of v1, /device:TPU:1, one launch (start us, length us, event | category | flops | bytes accessed | tf_op | source)
XLA Modules:
  0.0 229.2 jit_solution(8607432752919173582)
XLA Ops:
  1.3 0.0 copy-start
  1.3 1.4 copy-done
  2.7 0.0 copy-start.2
  2.7 1.2 copy-done.2
  3.9 0.0 copy-start.3
  3.9 0.7 copy-done.3
  4.6 0.0 copy-start.4
  4.6 0.7 copy-done.4
  5.3 0.0 copy-start.1
  5.3 9.3 %start.1 = (bf16[1024,1152]{1,0:T(8,128)(2,1)S(1)}, f32[9,128,128]{2,1,0:T(8,128)S(1)}) custom-call(f32[1]{0:T(128)S(6)} %copy.7.shift_ref, s32[1]{0:T(128)S(6)} %copy.8.split_ref, f32[8,128]{1,0:T(8,128)S(1)} %bitcast.32, s32[8,128]{1,0:T(8,128)S(1)} %bitcast.33, bf16[1024,768]{1,0:T(8,128)(2,1)S(1)} %copy-done, bf16[1024,512]{1,0:T(8,128)(2,1)S(1)} %copy-done.2), custom_call_target="tpu_custom_call" | custom-call | tf_op jit(solution)/shard_map/start/pallas_call | solution.py:182
  14.6 16.7 %share1.1 = (f32[18,64,128]{2,1,0:T(8,128)S(1)}, f32[18,64,128]{2,1,0:T(8,128)S(1)}) custom-call(f32[18,64,128]{2,1,0:T(8,128)S(1)} %bitcast.19), custom_call_target="tpu_custom_call" | custom-call | tf_op jit(solution)/shard_map/share1/pallas_call | solution.py:462
  31.3 0.0 copy-done.1
  31.3 4.8 %level1.1 = (bf16[1024,1024]{1,0:T(8,128)(2,1)S(1)}, f32[8,128,128]{2,1,0:T(8,128)S(1)}) custom-call(bf16[1024,1152]{1,0:T(8,128)(2,1)S(1)} %get-tuple-element.25.columns_ref, f32[9,128,128]{2,1,0:T(8,128)S(1)} %bitcast.17, f32[9,128,128]{2,1,0:T(8,128)S(1)} %bitcast.18, bf16[1024,768]{1,0:T(8,128)(2,1)S(1)} %copy-done.1), custom_call_target="tpu_custom_call" | custom-call | tf_op jit(solution)/shard_map/level1/pallas_call | solution.py:227
  36.2 25.7 %share2.1 = (f32[16,64,128]{2,1,0:T(8,128)S(1)}, f32[16,64,128]{2,1,0:T(8,128)S(1)}) custom-call(f32[16,64,128]{2,1,0:T(8,128)S(1)} %bitcast.22), custom_call_target="tpu_custom_call" | custom-call | tf_op jit(solution)/shard_map/share2/pallas_call | solution.py:462
  61.9 4.6 %level2.1 = (bf16[1024,896]{1,0:T(8,128)(2,1)S(1)}, f32[7,128,128]{2,1,0:T(8,128)S(1)}) custom-call(bf16[1024,1024]{1,0:T(8,128)(2,1)S(1)} %get-tuple-element.29.columns_ref, f32[8,128,128]{2,1,0:T(8,128)S(1)} %bitcast.20, f32[8,128,128]{2,1,0:T(8,128)S(1)} %bitcast.21, bf16[1024,768]{1,0:T(8,128)(2,1)S(1)} %copy-done.1), custom_call_target="tpu_custom_call" | custom-call | tf_op jit(solution)/shard_map/level2/pallas_call | solution.py:227
  66.5 33.5 %share3.1 = (f32[14,64,128]{2,1,0:T(8,128)S(1)}, f32[14,64,128]{2,1,0:T(8,128)S(1)}) custom-call(f32[14,64,128]{2,1,0:T(8,128)S(1)} %bitcast.25), custom_call_target="tpu_custom_call" | custom-call | tf_op jit(solution)/shard_map/share3/pallas_call | solution.py:462
  100.0 3.9 %level3.1 = (bf16[1024,768]{1,0:T(8,128)(2,1)S(1)}, f32[6,128,128]{2,1,0:T(8,128)S(1)}) custom-call(bf16[1024,896]{1,0:T(8,128)(2,1)S(1)} %get-tuple-element.33.columns_ref, f32[7,128,128]{2,1,0:T(8,128)S(1)} %bitcast.23, f32[7,128,128]{2,1,0:T(8,128)S(1)} %bitcast.24, bf16[1024,768]{1,0:T(8,128)(2,1)S(1)} %copy-done.1), custom_call_target="tpu_custom_call" | custom-call | tf_op jit(solution)/shard_map/level3/pallas_call | solution.py:227
  103.9 33.3 %share4.1 = (f32[12,64,128]{2,1,0:T(8,128)S(1)}, f32[12,64,128]{2,1,0:T(8,128)S(1)}) custom-call(f32[12,64,128]{2,1,0:T(8,128)S(1)} %bitcast.26), custom_call_target="tpu_custom_call" | custom-call | tf_op jit(solution)/shard_map/share4/pallas_call | solution.py:462
  137.2 3.7 %level4.1 = (bf16[1024,640]{1,0:T(8,128)(2,1)S(1)}, f32[5,128,128]{2,1,0:T(8,128)S(1)}) custom-call(bf16[1024,768]{1,0:T(8,128)(2,1)S(1)} %get-tuple-element.37.columns_ref, f32[6,128,128]{2,1,0:T(8,128)S(1)} %bitcast.27, f32[6,128,128]{2,1,0:T(8,128)S(1)} %bitcast.28, bf16[1024,768]{1,0:T(8,128)(2,1)S(1)} %copy-done.1), custom_call_target="tpu_custom_call" | custom-call | tf_op jit(solution)/shard_map/level4/pallas_call | solution.py:227
  141.0 84.5 %share5.1 = (f32[10,64,128]{2,1,0:T(8,128)S(1)}, f32[10,64,128]{2,1,0:T(8,128)S(1)}) custom-call(f32[10,64,128]{2,1,0:T(8,128)S(1)} %bitcast.31), custom_call_target="tpu_custom_call" | custom-call | tf_op jit(solution)/shard_map/share5/pallas_call | solution.py:462
  225.5 3.7 %level5.1 = bf16[1024,512]{1,0:T(8,128)(2,1)} custom-call(bf16[1024,640]{1,0:T(8,128)(2,1)S(1)} %get-tuple-element.41.columns_ref, f32[5,128,128]{2,1,0:T(8,128)S(1)} %bitcast.29, f32[5,128,128]{2,1,0:T(8,128)S(1)} %bitcast.30), custom_call_target="tpu_custom_call" | custom-call | tf_op jit(solution)/shard_map/level5/pallas_call | solution.py:227
Async XLA Ops:
  1.3 1.4 copy-start
  2.7 1.2 copy-start.2
  3.9 0.7 copy-start.3
  4.6 0.7 copy-start.4
  5.3 26.0 %copy-start.1 = (bf16[1024,768]{1,0:T(8,128)(2,1)S(1)}, bf16[1024,768]{1,0:T(8,128)(2,1)}, u32[]{:S(2)}) copy-start(bf16[1024,768]{1,0:T(8,128)(2,1)} %refs_0_.7) | copy-start | bytes 4718596

commit v2 on v1

v2 whole, which is shorter than its diff:
```python
import functools
import jax
import jax.numpy as jnp
from jax import lax
from jax.experimental import pallas as pl
from jax.experimental.pallas import tpu as pltpu
from jax.sharding import PartitionSpec as P

RANK = 128
PLANS = (("line", 384, 1), ("fold", 64, 8), ("fold", 128, 6), ("ring", 64, 12), ("core", 64, 9))
HIGHEST = lax.Precision.HIGHEST
VMEM = pltpu.VMEM


def dot32(a, b):
    return jnp.dot(a, b, precision=HIGHEST, preferred_element_type=jnp.float32)


def dot16(a, b):
    return jnp.dot(a, b, preferred_element_type=jnp.float32)


def halves(value):
    high = value.astype(jnp.bfloat16)
    return high, (value - high.astype(jnp.float32)).astype(jnp.bfloat16)


def store_mix(mix_ref, value):
    high, low = halves(value)
    depth = value.shape[1]
    mix_ref[:, pl.ds(0, depth)] = high
    mix_ref[:, pl.ds(depth, depth)] = high
    mix_ref[:, pl.ds(2 * depth, depth)] = low


def mixed(mix_ref, value):
    high, low = halves(value)
    return dot16(mix_ref[...], jnp.concatenate([high, low, high], axis=0))


def identity():
    shape = (RANK, RANK)
    rows = lax.broadcasted_iota(jnp.int32, shape, 0)
    cols = lax.broadcasted_iota(jnp.int32, shape, 1)
    return jnp.where(rows == cols, 1.0, 0.0).astype(jnp.float32)


def symmetric(value):
    return 0.5 * (value + value.T)


def invert(other, mine, inv_ref, pow_ref):
    step = dot32(other, mine)
    inv_ref[...] = identity() + step
    power = dot32(step, step)
    pow_ref[...] = power

    def unfinished(carry):
        count, size = carry
        return (count < 48) & (size > 1e-16)

    def more(carry):
        count, _ = carry
        inverse = inv_ref[...]
        power = pow_ref[...]
        inv_ref[...] = inverse + dot32(inverse, power)
        power = dot32(power, power)
        pow_ref[...] = power
        return count + 1, jnp.sum(power * power)

    lax.while_loop(unfinished, more, (jnp.int32(0), jnp.sum(power * power)))


def column_blocks(count, body):
    pairs = count // 2

    @pl.loop(0, pairs)
    def _(pair):
        body(2 * pair, 2)

    if count % 2:
        body(count - 1, 1)


def lanes(start, width):
    first = start * RANK
    if not isinstance(first, int):
        first = pl.multiple_of(first, RANK)
    return pl.ds(first, width * RANK)


def side_by_side(ref, first, width):
    return jnp.concatenate([ref[first + i] for i in range(width)], axis=1)


def update_blocks(columns_ref, left_of, coefs_of, next_ref, out_ref, partial_ref):
    count = out_ref.shape[1] // RANK

    def body(first, width):
        coef = coefs_of(first, width).astype(jnp.bfloat16)
        rest = columns_ref[:, lanes(first + 1, width)].astype(jnp.float32)
        fresh = (rest + dot16(left_of(), coef)).astype(jnp.bfloat16)
        out_ref[:, lanes(first, width)] = fresh
        if partial_ref is not None:
            sums = dot16(next_ref[...], fresh)
            for i in range(width):
                partial_ref[first + i] = sums[:, i * RANK : (i + 1) * RANK]

    column_blocks(count, body)


def start_kernel(
    shift_ref, split_ref, terms_ref, order_ref, coupling_ref, higher_ref,
    out_ref, partial_ref,
    columns_ref, own_ref, basis_t_ref, next_ref, sums_ref, mix_ref, inv_ref, pow_ref,
):
    rows, levels = coupling_ref.shape
    blocks = rows // RANK

    shift = shift_ref[0]
    split = split_ref[0]
    for block in range(blocks):
        here = pl.ds(block * RANK, RANK)
        diagonal = shift + terms_ref[pl.ds(block, 1), :]
        scale = jnp.broadcast_to(1.0 / diagonal, (RANK, RANK)).T
        mask = jnp.where(order_ref[pl.ds(block, 1), :] < split, 1.0, 0.0)
        inside_t = jnp.broadcast_to(mask, (RANK, RANK))
        inside = inside_t.T
        for first in range(0, levels, RANK):
            value = coupling_ref[here, pl.ds(first, RANK)].astype(jnp.float32)
            columns_ref[here, pl.ds(first, RANK)] = (value * scale).astype(jnp.bfloat16)
        own = columns_ref[here, pl.ds(0, RANK)].astype(jnp.float32)
        own_ref[here, pl.ds(0, RANK)] = (own * inside).astype(jnp.bfloat16)
        own_ref[here, pl.ds(RANK, RANK)] = (own * (1.0 - inside)).astype(jnp.bfloat16)
        basis_t = coupling_ref[here, pl.ds(0, RANK)].astype(jnp.float32).T
        basis_t_ref[pl.ds(0, RANK), here] = (basis_t * inside_t).astype(jnp.bfloat16)
        basis_t_ref[pl.ds(RANK, RANK), here] = (basis_t * (1.0 - inside_t)).astype(jnp.bfloat16)
        later = coupling_ref[here, pl.ds(RANK, RANK)].astype(jnp.float32)
        next_ref[:, here] = later.T.astype(jnp.bfloat16)
        for first in range(0, higher_ref.shape[1], RANK):
            value = higher_ref[here, pl.ds(first, RANK)].astype(jnp.float32)
            columns_ref[here, pl.ds(levels + first, RANK)] = (value * scale).astype(jnp.bfloat16)

    def project(first, width):
        sums_ref[:, lanes(first, width)] = dot16(
            basis_t_ref[...], columns_ref[:, lanes(first, width)]
        )

    column_blocks(columns_ref.shape[1] // RANK, project)
    first = symmetric(sums_ref[pl.ds(0, RANK), pl.ds(0, RANK)])
    second = symmetric(sums_ref[pl.ds(RANK, RANK), pl.ds(0, RANK)])
    invert(second, first, inv_ref, pow_ref)
    inverse = inv_ref[...]
    turned = inverse.T
    store_mix(
        mix_ref,
        jnp.concatenate(
            [
                jnp.concatenate([dot32(inverse, second), -inverse], axis=1),
                jnp.concatenate([-turned, dot32(turned, first)], axis=1),
            ],
            axis=0,
        ),
    )

    def coefs_of(first, width):
        return mixed(mix_ref, sums_ref[:, lanes(first + 1, width)])

    def left_of():
        return own_ref[...]

    update_blocks(columns_ref, left_of, coefs_of, next_ref, out_ref, partial_ref)


def level_kernel(level, last, folded, columns_ref, mine_ref, other_ref, *refs):
    if last:
        out_ref, mix_ref, inv_ref, pow_ref = refs
        partial_ref = next_ref = None
    else:
        coupling_ref, out_ref, partial_ref, mix_ref, inv_ref, pow_ref, next_ref = refs
        for block in range(coupling_ref.shape[0] // RANK):
            here = pl.ds(block * RANK, RANK)
            later = coupling_ref[here, pl.ds((level + 1) * RANK, RANK)].astype(jnp.float32)
            next_ref[:, here] = later.T.astype(jnp.bfloat16)
    mine = symmetric(mine_ref[0])
    other = symmetric(other_ref[0])
    invert(other, mine, inv_ref, pow_ref)
    inverse = inv_ref[...]
    beside = inverse if folded else -inverse
    store_mix(mix_ref, jnp.concatenate([dot32(inverse, other), beside], axis=1))

    def coefs_of(first, width):
        sums = jnp.concatenate(
            [side_by_side(mine_ref, first + 1, width), side_by_side(other_ref, first + 1, width)],
            axis=0,
        )
        return mixed(mix_ref, sums)

    def left_of():
        return columns_ref[:, pl.ds(0, RANK)]

    update_blocks(columns_ref, left_of, coefs_of, next_ref, out_ref, partial_ref)


def start_call(shift, split, terms, order, coupling, higher):
    rows, levels = coupling.shape
    width = levels + higher.shape[1]
    rest = width - RANK
    blocks = rows // RANK
    whole = pl.BlockSpec(memory_space=VMEM)
    scalar = pl.BlockSpec(memory_space=pltpu.SMEM)
    return pl.pallas_call(
        start_kernel,
        name="start",
        out_shape=(
            jax.ShapeDtypeStruct((rows, rest), jnp.bfloat16),
            jax.ShapeDtypeStruct((rest // RANK, RANK, RANK), jnp.float32),
        ),
        in_specs=[scalar, scalar, whole, whole, whole, whole],
        out_specs=(whole, whole),
        scratch_shapes=[
            VMEM((rows, width), jnp.bfloat16),
            VMEM((rows, 2 * RANK), jnp.bfloat16),
            VMEM((2 * RANK, rows), jnp.bfloat16),
            VMEM((RANK, rows), jnp.bfloat16),
            VMEM((2 * RANK, width), jnp.float32),
            VMEM((2 * RANK, 6 * RANK), jnp.bfloat16),
            VMEM((RANK, RANK), jnp.float32),
            VMEM((RANK, RANK), jnp.float32),
        ],
        compiler_params=pltpu.CompilerParams(vmem_limit_bytes=24 * 2**20),
    )(shift, split, terms.reshape(blocks, RANK), order.reshape(blocks, RANK), coupling, higher)


def level_call(level, folded, columns, mine, other, coupling):
    rows, width = columns.shape
    rest = width - RANK
    last = coupling is None
    out_shape = [jax.ShapeDtypeStruct((rows, rest), jnp.bfloat16)]
    scratch = [
        VMEM((RANK, 6 * RANK), jnp.bfloat16),
        VMEM((RANK, RANK), jnp.float32),
        VMEM((RANK, RANK), jnp.float32),
    ]
    operands = [columns, mine, other]
    if not last:
        out_shape.append(jax.ShapeDtypeStruct((rest // RANK, RANK, RANK), jnp.float32))
        scratch.append(VMEM((RANK, rows), jnp.bfloat16))
        operands.append(coupling)
    whole = pl.BlockSpec(memory_space=VMEM)
    return pl.pallas_call(
        functools.partial(level_kernel, level, last, folded),
        name=f"level{level}",
        out_shape=out_shape,
        in_specs=[whole] * len(operands),
        out_specs=[whole] * len(out_shape),
        scratch_shapes=scratch,
        compiler_params=pltpu.CompilerParams(vmem_limit_bytes=24 * 2**20),
    )(*operands)


def share_kernel(
    span, kind, pace, part_ref, mine_ref, other_ref,
    before, after, cross, up_buf, down_buf, half_ref, peer,
    before_sem, after_sem, cross_sem, up_sem, down_sem, pass_sem, swap_sem, trade_sem, peer_sem,
):
    chunks = part_ref.shape[0]
    place = lax.axis_index("sub")
    size = lax.axis_size("sub")
    leaf = lax.axis_index("leaf")
    above = {"sub": lax.rem(place + 1, size)}
    below = {"sub": lax.rem(place + size - 1, size)}
    partner = {"leaf": leaf + 1 - 2 * lax.rem(leaf, 2)}
    spot = lax.rem(place, span)
    first_child = lax.rem(place // span, 2) == 0
    has_below = spot > 0
    has_above = spot < span - 1
    barrier = pltpu.get_barrier_semaphore()
    if kind == "line":
        node_spot = lax.rem(place, 2 * span)
        link_below = node_spot > 0
        link_above = node_spot < 2 * span - 1

        @pl.when(link_above)
        def _():
            pl.semaphore_signal(barrier, inc=1, device_id=above)

        @pl.when(link_below)
        def _():
            pl.semaphore_signal(barrier, inc=1, device_id=below)

        pl.semaphore_wait(barrier, link_below.astype(jnp.int32) + link_above.astype(jnp.int32))
    else:
        pl.semaphore_signal(barrier, inc=1, device_id=below)
        pl.semaphore_signal(barrier, inc=1, device_id=above)
        if kind == "core":
            pl.semaphore_signal(barrier, inc=1, device_id=partner)
        pl.semaphore_wait(barrier, 3 if kind == "core" else 2)
    sum_ref = half_ref if kind == "core" else mine_ref

    def copy(src, dst, send, recv, c, to):
        return pltpu.make_async_remote_copy(
            src_ref=src.at[c], dst_ref=dst.at[c], send_sem=send.at[c], recv_sem=recv.at[c],
            device_id=to, device_id_type=pl.DeviceIdType.MESH,
        )

    def go_up(c):
        return copy(up_buf, before, up_sem, before_sem, c, above)

    def go_down(c):
        return copy(down_buf, after, down_sem, after_sem, c, below)

    def pass_on(c, to):
        return copy(cross, cross, pass_sem, cross_sem, c, to)

    def swap(c, to):
        return copy(sum_ref, cross, swap_sem, cross_sem, c, to)

    def trade(c):
        return copy(mine_ref, peer, trade_sem, peer_sem, c, partner)

    if kind == "line":
        reach = span
        distance = jnp.where(first_child, span - spot, spot + 1)
        forward_down = first_child & has_below
        forward_up = jnp.logical_not(first_child) & has_above
        swap_up = first_child & (spot == span - 1)
        swap_down = jnp.logical_not(first_child) & (spot == 0)
    else:
        reach = span // 2
        upper = spot >= reach
        distance = jnp.where(upper, span - spot, spot + 1)
        forward_down = upper & (spot > reach)
        forward_up = jnp.logical_not(upper) & (spot < reach - 1)
        swap_up = spot == span - 1
        swap_down = spot == 0
    up_from = pace * spot
    down_from = pace * (span - 1 - spot)
    sum_from = jnp.maximum(up_from, down_from)
    cross_from = pace * (span - 1 + distance)
    slots = chunks + pace * (span - 1 + reach)
    if kind == "core":
        slots += pace - 1

    def within(c):
        return (c >= 0) & (c < chunks)

    @pl.loop(0, slots)
    def _(slot):
        if span > 1:
            c = slot - up_from

            @pl.when(within(c))
            def _():
                @pl.when(has_below)
                def _():
                    go_up(c).wait_recv()

                @pl.when(has_above & has_below)
                def _():
                    up_buf[c] = part_ref[c] + before[c]

                @pl.when(has_above & jnp.logical_not(has_below))
                def _():
                    up_buf[c] = part_ref[c]

                @pl.when(has_above)
                def _():
                    go_up(c).start()

            d = slot - down_from

            @pl.when(within(d))
            def _():
                @pl.when(has_above)
                def _():
                    go_down(d).wait_recv()

                @pl.when(has_above & has_below)
                def _():
                    down_buf[d] = part_ref[d] + after[d]

                @pl.when(has_below & jnp.logical_not(has_above))
                def _():
                    down_buf[d] = part_ref[d]

                @pl.when(has_below)
                def _():
                    go_down(d).start()

        e = slot - sum_from

        @pl.when(within(e))
        def _():
            if span == 1:
                sum_ref[e] = part_ref[e]
            else:

                @pl.when(has_above & has_below)
                def _():
                    sum_ref[e] = part_ref[e] + before[e] + after[e]

                @pl.when(has_below & jnp.logical_not(has_above))
                def _():
                    sum_ref[e] = part_ref[e] + before[e]

                @pl.when(has_above & jnp.logical_not(has_below))
                def _():
                    sum_ref[e] = part_ref[e] + after[e]

            @pl.when(swap_up)
            def _():
                swap(e, above).start()

            @pl.when(swap_down)
            def _():
                swap(e, below).start()

        x = slot - cross_from

        @pl.when(within(x))
        def _():
            swap(x, above).wait_recv()
            if reach > 1:

                @pl.when(forward_up)
                def _():
                    pass_on(x, above).start()

                @pl.when(forward_down)
                def _():
                    pass_on(x, below).start()

            if kind == "core":
                mine_ref[x] = sum_ref[x] + cross[x]
                trade(x).start()
            else:
                other_ref[x] = cross[x]

        if kind == "core":
            y = slot - cross_from - (pace - 1)

            @pl.when(within(y))
            def _():
                trade(y).wait_recv()
                other_ref[y] = peer[y]

    @pl.loop(0, chunks)
    def _(c):
        if span > 1:

            @pl.when(has_above)
            def _():
                go_up(c).wait_send()

            @pl.when(has_below)
            def _():
                go_down(c).wait_send()

        @pl.when(swap_up | swap_down)
        def _():
            swap(c, above).wait_send()

        if reach > 1:

            @pl.when(forward_up | forward_down)
            def _():
                pass_on(c, above).wait_send()

        if kind == "core":
            trade(c).wait_send()


def fold_kernel(
    span, pace, part_ref, mine_ref, other_ref,
    before, after, cross, up_buf, down_buf, turned,
    before_sem, after_sem, cross_sem, up_sem, down_sem, pass_sem, swap_sem,
):
    chunks, height, _ = part_ref.shape
    head = RANK // height
    nodes = 2 * span
    place = lax.axis_index("sub")
    size = lax.axis_size("sub")
    above = {"sub": lax.rem(place + 1, size)}
    below = {"sub": lax.rem(place + size - 1, size)}
    spot = lax.rem(place, span)
    node_spot = lax.rem(place, nodes)
    first_child = node_spot < span
    second_child = jnp.logical_not(first_child)
    has_below = spot > 0
    has_above = spot < span - 1
    link_below = node_spot > 0
    link_above = node_spot < nodes - 1
    barrier = pltpu.get_barrier_semaphore()

    @pl.when(link_below)
    def _():
        pl.semaphore_signal(barrier, inc=1, device_id=below)

    @pl.when(link_above)
    def _():
        pl.semaphore_signal(barrier, inc=1, device_id=above)

    pl.semaphore_wait(barrier, link_below.astype(jnp.int32) + link_above.astype(jnp.int32))

    def copy(src, dst, send, recv, c, to):
        return pltpu.make_async_remote_copy(
            src_ref=src.at[c], dst_ref=dst.at[c], send_sem=send.at[c], recv_sem=recv.at[c],
            device_id=to, device_id_type=pl.DeviceIdType.MESH,
        )

    def go_up(c):
        return copy(up_buf, before, up_sem, before_sem, c, above)

    def go_down(c):
        return copy(down_buf, after, down_sem, after_sem, c, below)

    def pass_on(c, to):
        return copy(cross, cross, pass_sem, cross_sem, c, to)

    def swap(c, to):
        return copy(mine_ref, cross, swap_sem, cross_sem, c, to)

    forward_down = first_child & has_below
    forward_up = second_child & has_above
    swap_up = first_child & (spot == span - 1)
    swap_down = second_child & (spot == 0)
    distance = jnp.where(first_child, span - spot, spot + 1)
    cross_from = pace * (span - 1 + distance)
    up_from = pace * spot
    down_from = pace * (span - 1 - spot)
    sum_from = jnp.maximum(up_from, down_from)
    rise_from = pace * node_spot
    fall_from = pace * (nodes - 1 - node_spot)

    def in_head(c):
        return (c >= 0) & (c < head)

    def in_body(c):
        return (c >= head) & (c < chunks)

    @pl.loop(0, chunks + pace * (nodes - 1))
    def _(slot):
        c = slot - up_from

        @pl.when(in_head(c))
        def _():
            @pl.when(has_below)
            def _():
                go_up(c).wait_recv()

            @pl.when(has_above & has_below)
            def _():
                up_buf[c] = part_ref[c] + before[c]

            @pl.when(has_above & jnp.logical_not(has_below))
            def _():
                up_buf[c] = part_ref[c]

            @pl.when(has_above)
            def _():
                go_up(c).start()

        d = slot - down_from

        @pl.when(in_head(d))
        def _():
            @pl.when(has_above)
            def _():
                go_down(d).wait_recv()

            @pl.when(has_above & has_below)
            def _():
                down_buf[d] = part_ref[d] + after[d]

            @pl.when(has_below & jnp.logical_not(has_above))
            def _():
                down_buf[d] = part_ref[d]

            @pl.when(has_below)
            def _():
                go_down(d).start()

        e = slot - sum_from

        @pl.when(in_head(e))
        def _():
            @pl.when(has_above & has_below)
            def _():
                mine_ref[e] = part_ref[e] + before[e] + after[e]

            @pl.when(has_below & jnp.logical_not(has_above))
            def _():
                mine_ref[e] = part_ref[e] + before[e]

            @pl.when(has_above & jnp.logical_not(has_below))
            def _():
                mine_ref[e] = part_ref[e] + after[e]

            @pl.when(swap_up)
            def _():
                swap(e, above).start()

            @pl.when(swap_down)
            def _():
                swap(e, below).start()

        x = slot - cross_from

        @pl.when(in_head(x))
        def _():
            swap(x, above).wait_recv()

            @pl.when(forward_up)
            def _():
                pass_on(x, above).start()

            @pl.when(forward_down)
            def _():
                pass_on(x, below).start()

            other_ref[x] = cross[x]

        @pl.when((x == head - 1) & (forward_up | forward_down))
        def _():
            block = jnp.concatenate([cross[i] for i in range(head)], axis=0)
            for start in range(head, chunks, head):
                terms = jnp.concatenate([part_ref[start + i] for i in range(head)], axis=0)
                product = dot32(block, terms)
                for i in range(head):
                    turned[start + i] = product[i * height : (i + 1) * height, :]

        u = slot - rise_from

        @pl.when(in_body(u))
        def _():
            @pl.when(link_below)
            def _():
                go_up(u).wait_recv()

            @pl.when(first_child & jnp.logical_not(has_below))
            def _():
                value = part_ref[u]
                mine_ref[u] = value
                up_buf[u] = value

            @pl.when(first_child & has_below)
            def _():
                value = part_ref[u] + before[u]
                mine_ref[u] = value
                up_buf[u] = jnp.where(has_above, value, -value)

            @pl.when(second_child)
            def _():
                other_ref[u] = before[u]

            @pl.when(forward_up)
            def _():
                up_buf[u] = before[u] + turned[u]

            @pl.when(link_above)
            def _():
                go_up(u).start()

        v = slot - fall_from

        @pl.when(in_body(v))
        def _():
            @pl.when(link_above)
            def _():
                go_down(v).wait_recv()

            @pl.when(second_child & jnp.logical_not(has_above))
            def _():
                value = part_ref[v]
                mine_ref[v] = value
                down_buf[v] = value

            @pl.when(second_child & has_above)
            def _():
                value = part_ref[v] + after[v]
                mine_ref[v] = value
                down_buf[v] = jnp.where(has_below, value, -value)

            @pl.when(first_child)
            def _():
                other_ref[v] = after[v]

            @pl.when(forward_down)
            def _():
                down_buf[v] = after[v] + turned[v]

            @pl.when(link_below)
            def _():
                go_down(v).start()

    @pl.loop(0, head)
    def _(c):
        @pl.when(has_above)
        def _():
            go_up(c).wait_send()

        @pl.when(has_below)
        def _():
            go_down(c).wait_send()

        @pl.when(swap_up | swap_down)
        def _():
            swap(c, above).wait_send()

        @pl.when(forward_up | forward_down)
        def _():
            pass_on(c, above).wait_send()

    @pl.loop(head, chunks)
    def _(c):
        @pl.when(link_above)
        def _():
            go_up(c).wait_send()

        @pl.when(link_below)
        def _():
            go_down(c).wait_send()


def share_call(level, span, kind, height, pace, partial):
    blocks = partial.shape[0]
    chunks = blocks * RANK // height
    head = RANK // height
    shape = (chunks, height, RANK)
    whole = pl.BlockSpec(memory_space=VMEM)
    buffer = VMEM(shape, jnp.float32)
    semaphores = pltpu.SemaphoreType.DMA((chunks,))
    if kind == "fold":
        body = functools.partial(fold_kernel, span, pace)
        few = VMEM((head, height, RANK), jnp.float32)
        scratch = [buffer, buffer, few, buffer, buffer, buffer]
        some = pltpu.SemaphoreType.DMA((head,))
        scratch += [semaphores, semaphores, some, semaphores, semaphores, some, some]
    else:
        body = functools.partial(share_kernel, span, kind, pace)
        scratch = [buffer] * 7 + [semaphores] * 9
    mine, other = pl.pallas_call(
        body,
        name=f"share{level}",
        out_shape=(jax.ShapeDtypeStruct(shape, jnp.float32),) * 2,
        in_specs=[whole],
        out_specs=(whole, whole),
        scratch_shapes=scratch,
        compiler_params=pltpu.CompilerParams(
            collective_id=level, has_side_effects=True, vmem_limit_bytes=24 * 2**20
        ),
    )(partial.reshape(shape))
    full = (blocks, RANK, RANK)
    return mine.reshape(full), other.reshape(full)


def per_device(shift, self_terms, order, split, coupling, higher):
    size = lax.axis_size("sub")
    sub_bits = size.bit_length() - 1
    columns, partial = start_call(shift, split, self_terms, order[0], coupling, higher)
    for level in range(1, sub_bits + 1):
        span = 2 ** (level - 1)
        kind, height, pace = PLANS[level - 1]
        folded = kind == "fold"
        mine, other = share_call(level, span, kind, height, pace, partial)
        columns, partial = level_call(level, folded, columns, mine, other, coupling)
    kind, height, pace = PLANS[sub_bits]
    mine, other = share_call(sub_bits + 1, size // 2, kind, height, pace, partial)
    (columns,) = level_call(sub_bits + 1, False, columns, mine, other, None)
    return columns


def solution(mesh):
    in_specs = (
        P(),
        P(("leaf", "sub")),
        P(("leaf", "sub"), None),
        P(("leaf", "sub")),
        P(("leaf", "sub"), None),
        P(("leaf", "sub"), None),
    )
    out_specs = P(("leaf", "sub"), None)
    return jax.shard_map(
        per_device, mesh=mesh, in_specs=in_specs, out_specs=out_specs, check_vma=False
    )
```

time: 229 us -> 186 us (0.81)
  the two profiles are of different devices: /device:TPU:1 before, /device:TPU:127 now
where the time goes in v2:
time: 186 us
  Pallas kernels  180 us (97%)
  local copies, waits for them, and re-layouts  4 us (2%)
    pallas_call x5, Pallas kernels, share_call(): pl.pallas_call(body, name=f'share{level}', out_shape=(jax.ShapeDtypeStruc...  153 us
    pallas_call x5, Pallas kernels, level_call(): pl.pallas_call(functools.partial(level_kernel, level, last, folded), name...  19.2 us
    pallas_call x1, Pallas kernels, start_call(): pl.pallas_call(start_kernel, name='start', out_shape=(jax.ShapeDtypeStruc...  8.18 us
    unnamed x10, local copies, waits for them, and re-layouts  4 us

profile of v2, /device:TPU:127, one launch (start us, length us, event | category | flops | bytes accessed | tf_op | source)
XLA Modules:
  0.0 185.8 jit_solution(4320873700266537684)
XLA Ops:
  1.3 0.0 copy-start
  1.3 1.4 copy-done
  2.7 0.0 copy-start.2
  2.7 1.2 copy-done.2
  3.9 0.0 copy-start.3
  3.9 0.7 copy-done.3
  4.6 0.0 copy-start.4
  4.6 0.7 copy-done.4
  5.3 0.0 copy-start.1
  5.3 8.2 %start.1 = (bf16[1024,1152]{1,0:T(8,128)(2,1)S(1)}, f32[9,128,128]{2,1,0:T(8,128)S(1)}) custom-call(f32[1]{0:T(128)S(6)} %copy.7.shift_ref, s32[1]{0:T(128)S(6)} %copy.8.split_ref, f32[8,128]{1,0:T(8,128)S(1)} %bitcast.26, s32[8,128]{1,0:T(8,128)S(1)} %bitcast.27, bf16[1024,768]{1,0:T(8,128)(2,1)S(1)} %copy-done, bf16[1024,512]{1,0:T(8,128)(2,1)S(1)} %copy-done.2), custom_call_target="tpu_custom_call" | custom-call | tf_op jit(solution)/shard_map/start/pallas_call | solution.py:212
  13.5 15.2 %share1.1 = (f32[3,384,128]{2,1,0:T(8,128)S(1)}, f32[3,384,128]{2,1,0:T(8,128)S(1)}) custom-call(f32[3,384,128]{2,1,0:T(8,128)S(1)} %bitcast.16), custom_call_target="tpu_custom_call" | custom-call | tf_op jit(solution)/shard_map/share1/pallas_call | solution.py:743
  28.7 0.0 copy-done.1
  28.7 4.5 %level1.1 = (bf16[1024,1024]{1,0:T(8,128)(2,1)S(1)}, f32[8,128,128]{2,1,0:T(8,128)S(1)}) custom-call(bf16[1024,1152]{1,0:T(8,128)(2,1)S(1)} %get-tuple-element.25.columns_ref, f32[9,128,128]{2,1,0:T(8,128)S(1)} %bitcast.14, f32[9,128,128]{2,1,0:T(8,128)S(1)} %bitcast.15, bf16[1024,768]{1,0:T(8,128)(2,1)S(1)} %copy-done.1), custom_call_target="tpu_custom_call" | custom-call | tf_op jit(solution)/shard_map/level1/pallas_call | solution.py:251
  33.2 20.7 %share2.1 = (f32[16,64,128]{2,1,0:T(8,128)S(1)}, f32[16,64,128]{2,1,0:T(8,128)S(1)}) custom-call(f32[16,64,128]{2,1,0:T(8,128)S(1)} %bitcast.19), custom_call_target="tpu_custom_call" | custom-call | tf_op jit(solution)/shard_map/share2/pallas_call | solution.py:743
  53.9 4.2 %level2.1 = (bf16[1024,896]{1,0:T(8,128)(2,1)S(1)}, f32[7,128,128]{2,1,0:T(8,128)S(1)}) custom-call(bf16[1024,1024]{1,0:T(8,128)(2,1)S(1)} %get-tuple-element.29.columns_ref, f32[8,128,128]{2,1,0:T(8,128)S(1)} %bitcast.17, f32[8,128,128]{2,1,0:T(8,128)S(1)} %bitcast.18, bf16[1024,768]{1,0:T(8,128)(2,1)S(1)} %copy-done.1), custom_call_target="tpu_custom_call" | custom-call | tf_op jit(solution)/shard_map/level2/pallas_call | solution.py:251
  58.1 25.7 %share3.1 = (f32[7,128,128]{2,1,0:T(8,128)S(1)}, f32[7,128,128]{2,1,0:T(8,128)S(1)}) custom-call(f32[7,128,128]{2,1,0:T(8,128)S(1)} %get-tuple-element.34.part_ref), custom_call_target="tpu_custom_call" | custom-call | tf_op jit(solution)/shard_map/share3/pallas_call | solution.py:743
  83.9 3.7 %level3.1 = (bf16[1024,768]{1,0:T(8,128)(2,1)S(1)}, f32[6,128,128]{2,1,0:T(8,128)S(1)}) custom-call(bf16[1024,896]{1,0:T(8,128)(2,1)S(1)} %get-tuple-element.33.columns_ref, f32[7,128,128]{2,1,0:T(8,128)S(1)} %get-tuple-element.35.mine_ref, f32[7,128,128]{2,1,0:T(8,128)S(1)} %get-tuple-element.36.other_ref, bf16[1024,768]{1,0:T(8,128)(2,1)S(1)} %copy-done.1), custom_call_target="tpu_custom_call" | custom-call | tf_op jit(solution)/shard_map/level3/pallas_call | solution.py:251
  87.5 41.7 %share4.1 = (f32[12,64,128]{2,1,0:T(8,128)S(1)}, f32[12,64,128]{2,1,0:T(8,128)S(1)}) custom-call(f32[12,64,128]{2,1,0:T(8,128)S(1)} %bitcast.20), custom_call_target="tpu_custom_call" | custom-call | tf_op jit(solution)/shard_map/share4/pallas_call | solution.py:743
  129.3 3.4 %level4.1 = (bf16[1024,640]{1,0:T(8,128)(2,1)S(1)}, f32[5,128,128]{2,1,0:T(8,128)S(1)}) custom-call(bf16[1024,768]{1,0:T(8,128)(2,1)S(1)} %get-tuple-element.37.columns_ref, f32[6,128,128]{2,1,0:T(8,128)S(1)} %bitcast.21, f32[6,128,128]{2,1,0:T(8,128)S(1)} %bitcast.22, bf16[1024,768]{1,0:T(8,128)(2,1)S(1)} %copy-done.1), custom_call_target="tpu_custom_call" | custom-call | tf_op jit(solution)/shard_map/level4/pallas_call | solution.py:251
  132.7 49.7 %share5.1 = (f32[10,64,128]{2,1,0:T(8,128)S(1)}, f32[10,64,128]{2,1,0:T(8,128)S(1)}) custom-call(f32[10,64,128]{2,1,0:T(8,128)S(1)} %bitcast.25), custom_call_target="tpu_custom_call" | custom-call | tf_op jit(solution)/shard_map/share5/pallas_call | solution.py:743
  182.4 3.4 %level5.1 = bf16[1024,512]{1,0:T(8,128)(2,1)} custom-call(bf16[1024,640]{1,0:T(8,128)(2,1)S(1)} %get-tuple-element.41.columns_ref, f32[5,128,128]{2,1,0:T(8,128)S(1)} %bitcast.23, f32[5,128,128]{2,1,0:T(8,128)S(1)} %bitcast.24), custom_call_target="tpu_custom_call" | custom-call | tf_op jit(solution)/shard_map/level5/pallas_call | solution.py:251
Async XLA Ops:
  1.3 1.4 copy-start
  2.7 1.2 copy-start.2
  3.9 0.7 copy-start.3
  4.6 0.7 copy-start.4
  5.3 23.4 %copy-start.1 = (bf16[1024,768]{1,0:T(8,128)(2,1)S(1)}, bf16[1024,768]{1,0:T(8,128)(2,1)}, u32[]{:S(2)}) copy-start(bf16[1024,768]{1,0:T(8,128)(2,1)} %refs_0_.7) | copy-start | bytes 4718596

commit v3 on v2

--- a/solution.py
+++ b/solution.py
@@ -7,7 +7,13 @@
 from jax.sharding import PartitionSpec as P
 
 RANK = 128
-PLANS = (("line", 384, 1), ("fold", 64, 8), ("fold", 128, 6), ("ring", 64, 12), ("core", 64, 9))
+PLANS = (
+    ("line", 384, 3, 3),
+    ("fold", 128, 4, 2),
+    ("fold", 64, 12, 2),
+    ("ring", 64, 8, 2),
+    ("core", 64, 9, 2),
+)
 HIGHEST = lax.Precision.HIGHEST
 VMEM = pltpu.VMEM
 
@@ -93,26 +99,92 @@
     return jnp.concatenate([ref[first + i] for i in range(width)], axis=1)
 
 
-def update_blocks(columns_ref, left_of, coefs_of, next_ref, out_ref, partial_ref):
-    count = out_ref.shape[1] // RANK
-
-    def body(first, width):
-        coef = coefs_of(first, width).astype(jnp.bfloat16)
-        rest = columns_ref[:, lanes(first + 1, width)].astype(jnp.float32)
-        fresh = (rest + dot16(left_of(), coef)).astype(jnp.bfloat16)
-        out_ref[:, lanes(first, width)] = fresh
-        if partial_ref is not None:
-            sums = dot16(next_ref[...], fresh)
-            for i in range(width):
-                partial_ref[first + i] = sums[:, i * RANK : (i + 1) * RANK]
-
-    column_blocks(count, body)
+def update(columns_ref, left_of, coefs_of, out_ref, first, width):
+    coef = coefs_of(first, width).astype(jnp.bfloat16)
+    rest = columns_ref[:, lanes(first + 1, width)].astype(jnp.float32)
+    fresh = (rest + dot16(left_of(), coef)).astype(jnp.bfloat16)
+    out_ref[:, lanes(first, width)] = fresh
+    return fresh
+
+
+def level_coefs(mine_ref, other_ref, mix_ref):
+    def coefs_of(first, width):
+        sums = jnp.concatenate(
+            [side_by_side(mine_ref, first + 1, width), side_by_side(other_ref, first + 1, width)],
+            axis=0,
+        )
+        return mixed(mix_ref, sums)
+
+    return coefs_of
+
+
+def solve(mine_ref, other_ref, folded, mix_ref, inv_ref, pow_ref):
+    mine = symmetric(mine_ref[0])
+    other = symmetric(other_ref[0])
+    invert(other, mine, inv_ref, pow_ref)
+    inverse = inv_ref[...]
+    beside = inverse if folded else -inverse
+    store_mix(mix_ref, jnp.concatenate([dot32(inverse, other), beside], axis=1))
+
+
+def updates_in(share, level, height, wide, *refs):
+    columns_ref, near_ref, far_ref, mix_ref, coupling_ref, out_ref, mine_ref, other_ref = refs[:8]
+    next_ref, part_ref = refs[8:10]
+    blocks = out_ref.shape[1] // RANK
+    steps = wide * RANK // height
+    full = blocks // wide
+    if level == 1:
+
+        def coefs_of(first, width):
+            return mixed(mix_ref, far_ref[:, lanes(first + 1, width)])
+
+        def left_of():
+            return near_ref[...]
+
+    else:
+        coefs_of = level_coefs(near_ref, far_ref, mix_ref)
+
+        def left_of():
+            return columns_ref[:, pl.ds(0, RANK)]
+
+    def prepare():
+        for block in range(coupling_ref.shape[0] // RANK):
+            here = pl.ds(block * RANK, RANK)
+            later = coupling_ref[here, pl.ds(level * RANK, RANK)].astype(jnp.float32)
+            next_ref[:, here] = later.T.astype(jnp.bfloat16)
+
+    def make(step, width):
+        first = step * wide
+        fresh = update(columns_ref, left_of, coefs_of, out_ref, first, width)
+        sums = dot16(next_ref[...], fresh)
+        for i in range(width):
+            block = sums[:, i * RANK : (i + 1) * RANK]
+            if height > RANK:
+                part_ref[step, pl.ds(i * RANK, RANK), :] = block
+            else:
+                pieces = RANK // height
+                for piece in range(pieces):
+                    rows = block[piece * height : (piece + 1) * height, :]
+                    part_ref[(first + i) * pieces + piece] = rows
+
+    def ready(slot):
+        @pl.when((lax.rem(slot, steps) == 0) & (slot < full * steps))
+        def _():
+            make(slot // steps, wide)
+
+        if blocks % wide:
+
+            @pl.when(slot == full * steps)
+            def _():
+                make(full, blocks % wide)
+
+    share(prepare, ready, part_ref, mine_ref, other_ref, *refs[10:])
 
 
 def start_kernel(
     shift_ref, split_ref, terms_ref, order_ref, coupling_ref, higher_ref,
-    out_ref, partial_ref,
-    columns_ref, own_ref, basis_t_ref, next_ref, sums_ref, mix_ref, inv_ref, pow_ref,
+    columns_ref, own_ref, sums_ref, mix_ref,
+    basis_t_ref, inv_ref, pow_ref,
 ):
     rows, levels = coupling_ref.shape
     blocks = rows // RANK
@@ -135,8 +207,6 @@
         basis_t = coupling_ref[here, pl.ds(0, RANK)].astype(jnp.float32).T
         basis_t_ref[pl.ds(0, RANK), here] = (basis_t * inside_t).astype(jnp.bfloat16)
         basis_t_ref[pl.ds(RANK, RANK), here] = (basis_t * (1.0 - inside_t)).astype(jnp.bfloat16)
-        later = coupling_ref[here, pl.ds(RANK, RANK)].astype(jnp.float32)
-        next_ref[:, here] = later.T.astype(jnp.bfloat16)
         for first in range(0, higher_ref.shape[1], RANK):
             value = higher_ref[here, pl.ds(first, RANK)].astype(jnp.float32)
             columns_ref[here, pl.ds(levels + first, RANK)] = (value * scale).astype(jnp.bfloat16)
@@ -163,49 +233,27 @@
         ),
     )
 
-    def coefs_of(first, width):
-        return mixed(mix_ref, sums_ref[:, lanes(first + 1, width)])
-
-    def left_of():
-        return own_ref[...]
-
-    update_blocks(columns_ref, left_of, coefs_of, next_ref, out_ref, partial_ref)
-
-
-def level_kernel(level, last, folded, columns_ref, mine_ref, other_ref, *refs):
-    if last:
-        out_ref, mix_ref, inv_ref, pow_ref = refs
-        partial_ref = next_ref = None
-    else:
-        coupling_ref, out_ref, partial_ref, mix_ref, inv_ref, pow_ref, next_ref = refs
-        for block in range(coupling_ref.shape[0] // RANK):
-            here = pl.ds(block * RANK, RANK)
-            later = coupling_ref[here, pl.ds((level + 1) * RANK, RANK)].astype(jnp.float32)
-            next_ref[:, here] = later.T.astype(jnp.bfloat16)
-    mine = symmetric(mine_ref[0])
-    other = symmetric(other_ref[0])
-    invert(other, mine, inv_ref, pow_ref)
-    inverse = inv_ref[...]
-    beside = inverse if folded else -inverse
-    store_mix(mix_ref, jnp.concatenate([dot32(inverse, other), beside], axis=1))
-
-    def coefs_of(first, width):
-        sums = jnp.concatenate(
-            [side_by_side(mine_ref, first + 1, width), side_by_side(other_ref, first + 1, width)],
-            axis=0,
-        )
-        return mixed(mix_ref, sums)
+
+def solve_kernel(folded, mine_ref, other_ref, mix_ref, inv_ref, pow_ref):
+    solve(mine_ref, other_ref, folded, mix_ref, inv_ref, pow_ref)
+
+
+def last_kernel(columns_ref, mine_ref, other_ref, out_ref, mix_ref, inv_ref, pow_ref):
+    solve(mine_ref, other_ref, False, mix_ref, inv_ref, pow_ref)
+    coefs_of = level_coefs(mine_ref, other_ref, mix_ref)
 
     def left_of():
         return columns_ref[:, pl.ds(0, RANK)]
 
-    update_blocks(columns_ref, left_of, coefs_of, next_ref, out_ref, partial_ref)
+    def body(first, width):
+        update(columns_ref, left_of, coefs_of, out_ref, first, width)
+
+    column_blocks(out_ref.shape[1] // RANK, body)
 
 
 def start_call(shift, split, terms, order, coupling, higher):
     rows, levels = coupling.shape
     width = levels + higher.shape[1]
-    rest = width - RANK
     blocks = rows // RANK
     whole = pl.BlockSpec(memory_space=VMEM)
     scalar = pl.BlockSpec(memory_space=pltpu.SMEM)
@@ -213,18 +261,15 @@
         start_kernel,
         name="start",
         out_shape=(
-            jax.ShapeDtypeStruct((rows, rest), jnp.bfloat16),
-            jax.ShapeDtypeStruct((rest // RANK, RANK, RANK), jnp.float32),
+            jax.ShapeDtypeStruct((rows, width), jnp.bfloat16),
+            jax.ShapeDtypeStruct((rows, 2 * RANK), jnp.bfloat16),
+            jax.ShapeDtypeStruct((2 * RANK, width), jnp.float32),
+            jax.ShapeDtypeStruct((2 * RANK, 6 * RANK), jnp.bfloat16),
         ),
         in_specs=[scalar, scalar, whole, whole, whole, whole],
-        out_specs=(whole, whole),
+        out_specs=(whole,) * 4,
         scratch_shapes=[
-            VMEM((rows, width), jnp.bfloat16),
-            VMEM((rows, 2 * RANK), jnp.bfloat16),
             VMEM((2 * RANK, rows), jnp.bfloat16),
-            VMEM((RANK, rows), jnp.bfloat16),
-            VMEM((2 * RANK, width), jnp.float32),
-            VMEM((2 * RANK, 6 * RANK), jnp.bfloat16),
             VMEM((RANK, RANK), jnp.float32),
             VMEM((RANK, RANK), jnp.float32),
         ],
@@ -232,35 +277,37 @@
     )(shift, split, terms.reshape(blocks, RANK), order.reshape(blocks, RANK), coupling, higher)
 
 
-def level_call(level, folded, columns, mine, other, coupling):
-    rows, width = columns.shape
-    rest = width - RANK
-    last = coupling is None
-    out_shape = [jax.ShapeDtypeStruct((rows, rest), jnp.bfloat16)]
-    scratch = [
-        VMEM((RANK, 6 * RANK), jnp.bfloat16),
-        VMEM((RANK, RANK), jnp.float32),
-        VMEM((RANK, RANK), jnp.float32),
-    ]
-    operands = [columns, mine, other]
-    if not last:
-        out_shape.append(jax.ShapeDtypeStruct((rest // RANK, RANK, RANK), jnp.float32))
-        scratch.append(VMEM((RANK, rows), jnp.bfloat16))
-        operands.append(coupling)
+def solve_call(level, folded, mine, other):
+    square = VMEM((RANK, RANK), jnp.float32)
     whole = pl.BlockSpec(memory_space=VMEM)
     return pl.pallas_call(
-        functools.partial(level_kernel, level, last, folded),
-        name=f"level{level}",
-        out_shape=out_shape,
-        in_specs=[whole] * len(operands),
-        out_specs=[whole] * len(out_shape),
-        scratch_shapes=scratch,
+        functools.partial(solve_kernel, folded),
+        name=f"solve{level}",
+        out_shape=jax.ShapeDtypeStruct((RANK, 6 * RANK), jnp.bfloat16),
+        in_specs=[whole, whole],
+        out_specs=whole,
+        scratch_shapes=[square, square],
+        compiler_params=pltpu.CompilerParams(vmem_limit_bytes=8 * 2**20),
+    )(mine, other)
+
+
+def last_call(columns, mine, other):
+    rows, width = columns.shape
+    square = VMEM((RANK, RANK), jnp.float32)
+    whole = pl.BlockSpec(memory_space=VMEM)
+    return pl.pallas_call(
+        last_kernel,
+        name="last",
+        out_shape=jax.ShapeDtypeStruct((rows, width - RANK), jnp.bfloat16),
+        in_specs=[whole] * 3,
+        out_specs=whole,
+        scratch_shapes=[VMEM((RANK, 6 * RANK), jnp.bfloat16), square, square],
         compiler_params=pltpu.CompilerParams(vmem_limit_bytes=24 * 2**20),
-    )(*operands)
+    )(columns, mine, other)
 
 
 def share_kernel(
-    span, kind, pace, part_ref, mine_ref, other_ref,
+    span, kind, pace, prepare, ready, part_ref, mine_ref, other_ref,
     before, after, cross, up_buf, down_buf, half_ref, peer,
     before_sem, after_sem, cross_sem, up_sem, down_sem, pass_sem, swap_sem, trade_sem, peer_sem,
 ):
@@ -289,12 +336,14 @@
         def _():
             pl.semaphore_signal(barrier, inc=1, device_id=below)
 
+        prepare()
         pl.semaphore_wait(barrier, link_below.astype(jnp.int32) + link_above.astype(jnp.int32))
     else:
         pl.semaphore_signal(barrier, inc=1, device_id=below)
         pl.semaphore_signal(barrier, inc=1, device_id=above)
         if kind == "core":
             pl.semaphore_signal(barrier, inc=1, device_id=partner)
+        prepare()
         pl.semaphore_wait(barrier, 3 if kind == "core" else 2)
     sum_ref = half_ref if kind == "core" else mine_ref
 
@@ -347,6 +396,7 @@
 
     @pl.loop(0, slots)
     def _(slot):
+        ready(slot)
         if span > 1:
             c = slot - up_from
 
@@ -472,7 +522,7 @@
 
 
 def fold_kernel(
-    span, pace, part_ref, mine_ref, other_ref,
+    span, pace, prepare, ready, part_ref, mine_ref, other_ref,
     before, after, cross, up_buf, down_buf, turned,
     before_sem, after_sem, cross_sem, up_sem, down_sem, pass_sem, swap_sem,
 ):
@@ -501,6 +551,7 @@
     def _():
         pl.semaphore_signal(barrier, inc=1, device_id=above)
 
+    prepare()
     pl.semaphore_wait(barrier, link_below.astype(jnp.int32) + link_above.astype(jnp.int32))
 
     def copy(src, dst, send, recv, c, to):
@@ -541,6 +592,7 @@
 
     @pl.loop(0, chunks + pace * (nodes - 1))
     def _(slot):
+        ready(slot)
         c = slot - up_from
 
         @pl.when(in_head(c))
@@ -723,52 +775,55 @@
             go_down(c).wait_send()
 
 
-def share_call(level, span, kind, height, pace, partial):
-    blocks = partial.shape[0]
-    chunks = blocks * RANK // height
+def share_call(level, span, columns, near, far, mix, coupling):
+    kind, height, pace, wide = PLANS[level - 1]
+    rows, width = columns.shape
+    rest = width - RANK
+    blocks = rest // RANK
+    chunks = rest // height
     head = RANK // height
     shape = (chunks, height, RANK)
     whole = pl.BlockSpec(memory_space=VMEM)
     buffer = VMEM(shape, jnp.float32)
     semaphores = pltpu.SemaphoreType.DMA((chunks,))
     if kind == "fold":
-        body = functools.partial(fold_kernel, span, pace)
+        share = functools.partial(fold_kernel, span, pace)
         few = VMEM((head, height, RANK), jnp.float32)
+        some = pltpu.SemaphoreType.DMA((head,))
         scratch = [buffer, buffer, few, buffer, buffer, buffer]
-        some = pltpu.SemaphoreType.DMA((head,))
         scratch += [semaphores, semaphores, some, semaphores, semaphores, some, some]
     else:
-        body = functools.partial(share_kernel, span, kind, pace)
+        share = functools.partial(share_kernel, span, kind, pace)
         scratch = [buffer] * 7 + [semaphores] * 9
-    mine, other = pl.pallas_call(
-        body,
+    columns, mine, other = pl.pallas_call(
+        functools.partial(updates_in, share, level, height, wide),
         name=f"share{level}",
-        out_shape=(jax.ShapeDtypeStruct(shape, jnp.float32),) * 2,
-        in_specs=[whole],
-        out_specs=(whole, whole),
-        scratch_shapes=scratch,
+        out_shape=(
+            jax.ShapeDtypeStruct((rows, rest), jnp.bfloat16),
+            jax.ShapeDtypeStruct(shape, jnp.float32),
+            jax.ShapeDtypeStruct(shape, jnp.float32),
+        ),
+        in_specs=[whole] * 5,
+        out_specs=(whole,) * 3,
+        scratch_shapes=[VMEM((RANK, rows), jnp.bfloat16), buffer] + scratch,
         compiler_params=pltpu.CompilerParams(
             collective_id=level, has_side_effects=True, vmem_limit_bytes=24 * 2**20
         ),
-    )(partial.reshape(shape))
-    full = (blocks, RANK, RANK)
-    return mine.reshape(full), other.reshape(full)
+    )(columns, near, far, mix, coupling)
+    squares = (blocks, RANK, RANK)
+    return columns, mine.reshape(squares), other.reshape(squares)
 
 
 def per_device(shift, self_terms, order, split, coupling, higher):
     size = lax.axis_size("sub")
-    sub_bits = size.bit_length() - 1
-    columns, partial = start_call(shift, split, self_terms, order[0], coupling, higher)
-    for level in range(1, sub_bits + 1):
-        span = 2 ** (level - 1)
-        kind, height, pace = PLANS[level - 1]
-        folded = kind == "fold"
-        mine, other = share_call(level, span, kind, height, pace, partial)
-        columns, partial = level_call(level, folded, columns, mine, other, coupling)
-    kind, height, pace = PLANS[sub_bits]
-    mine, other = share_call(sub_bits + 1, size // 2, kind, height, pace, partial)
-    (columns,) = level_call(sub_bits + 1, False, columns, mine, other, None)
-    return columns
+    columns, near, far, mix = start_call(shift, split, self_terms, order[0], coupling, higher)
+    for level in range(1, len(PLANS) + 1):
+        kind = PLANS[level - 1][0]
+        span = min(2 ** (level - 1), size // 2)
+        columns, near, far = share_call(level, span, columns, near, far, mix, coupling)
+        if level < len(PLANS):
+            mix = solve_call(level, kind == "fold", near, far)
+    return last_call(columns, near, far)
 
 
 def solution(mesh):

time: 186 us -> 178 us (0.957)
  the two profiles are of different devices: /device:TPU:127 before, /device:TPU:109 now
where the time goes in v3:
time: 178 us
  Pallas kernels  172 us (97%)
  local copies, waits for them, and re-layouts  4 us (2%)
    pallas_call x5, Pallas kernels, share_call(): pl.pallas_call(functools.partial(updates_in, share, level, height, wide),...  160 us
    pallas_call x4, Pallas kernels, solve_call(): pl.pallas_call(functools.partial(solve_kernel, folded), name=f'solve{leve...  4.96 us
    pallas_call x1, Pallas kernels, start_call(): pl.pallas_call(start_kernel, name='start', out_shape=(jax.ShapeDtypeStruc...  4.13 us
    unnamed x10, local copies, waits for them, and re-layouts  4 us

profile of v3, /device:TPU:109, one launch (start us, length us, event | category | flops | bytes accessed | tf_op | source)
XLA Modules:
  0.0 177.7 jit_solution(6654570899224144114)
XLA Ops:
  1.3 0.0 copy-start
  1.3 1.4 copy-done
  2.7 0.0 copy-start.2
  2.7 1.2 copy-done.2
  3.9 0.0 copy-start.3
  3.9 0.7 copy-done.3
  4.6 0.0 copy-start.4
  4.6 0.7 copy-done.4
  5.3 0.0 copy-start.1
  5.3 4.1 %start.1 = (bf16[1024,1280]{1,0:T(8,128)(2,1)S(1)}, bf16[1024,256]{1,0:T(8,128)(2,1)S(1)}, f32[256,1280]{1,0:T(8,128)S(1)}, bf16[256,768]{1,0:T(8,128)(2,1)S(1)}) custom-call(f32[1]{0:T(128)S(6)} %copy.7.shift_ref, s32[1]{0:T(128)S(6)} %copy.8.split_ref, f32[8,128]{1,0:T(8,128)S(1)} %bitcast.24, s32[8,128]{1,0:T(8,128)S(1)} %bitcast.25, ...), custom_call_target="tpu_custom_call" | custom-call | tf_op jit(solution)/shard_map/start/pallas_call | solution.py:260
  9.4 0.0 copy-done.1
  9.5 16.5 %share1.1 = (bf16[1024,1152]{1,0:T(8,128)(2,1)S(1)}, f32[3,384,128]{2,1,0:T(8,128)S(1)}, f32[3,384,128]{2,1,0:T(8,128)S(1)}) custom-call(bf16[1024,1280]{1,0:T(8,128)(2,1)S(1)} %get-tuple-element.24.refs_0_, bf16[1024,256]{1,0:T(8,128)(2,1)S(1)} %get-tuple-element.25.refs_1_, f32[256,1280]{1,0:T(8,128)S(1)} %get-tuple-element.26.refs_2_, ...), custom_call_target="tpu_custom_call" | custom-call | tf_op jit(solution)/shard_map/share1/pallas_call | solution.py:798
  26.0 1.2 solve1.1.refs_3_
  27.2 21.2 %share2.1 = (bf16[1024,1024]{1,0:T(8,128)(2,1)S(1)}, f32[8,128,128]{2,1,0:T(8,128)S(1)}, f32[8,128,128]{2,1,0:T(8,128)S(1)}) custom-call(bf16[1024,1152]{1,0:T(8,128)(2,1)S(1)} %get-tuple-element.28.refs_0_, f32[9,128,128]{2,1,0:T(8,128)S(1)} %bitcast.11, f32[9,128,128]{2,1,0:T(8,128)S(1)} %bitcast.13, bf16[128,768]{1,0:T(8,128)(2,1)S(1)} %solve1.1.refs_3_, ...), custom_call_target="tpu_custom_call" | custom-call | tf_op jit(solution)/shard_map/share2/pallas_call | solution.py:798
  48.4 1.2 solve2.1.refs_3_
  49.6 25.9 %share3.1 = (bf16[1024,896]{1,0:T(8,128)(2,1)S(1)}, f32[14,64,128]{2,1,0:T(8,128)S(1)}, f32[14,64,128]{2,1,0:T(8,128)S(1)}) custom-call(bf16[1024,1024]{1,0:T(8,128)(2,1)S(1)} %get-tuple-element.31.refs_0_, f32[8,128,128]{2,1,0:T(8,128)S(1)} %get-tuple-element.32.mine_ref.refs_1_, f32[8,128,128]{2,1,0:T(8,128)S(1)} %get-tuple-element.33.other_ref.refs_2_, ...), custom_call_target="tpu_custom_call" | custom-call | tf_op jit(solution)/shard_map/share3/pallas_call | solution.py:798
  75.6 1.2 solve3.1.refs_3_
  76.8 41.9 %share4.1 = (bf16[1024,768]{1,0:T(8,128)(2,1)S(1)}, f32[12,64,128]{2,1,0:T(8,128)S(1)}, f32[12,64,128]{2,1,0:T(8,128)S(1)}) custom-call(bf16[1024,896]{1,0:T(8,128)(2,1)S(1)} %get-tuple-element.34.refs_0_, f32[7,128,128]{2,1,0:T(8,128)S(1)} %bitcast.15, f32[7,128,128]{2,1,0:T(8,128)S(1)} %bitcast.17, bf16[128,768]{1,0:T(8,128)(2,1)S(1)} %solve3.1.refs_3_, ...), custom_call_target="tpu_custom_call" | custom-call | tf_op jit(solution)/shard_map/share4/pallas_call | solution.py:798
  118.7 1.2 solve4.1.refs_3_
  120.0 54.4 %share5.1 = (bf16[1024,640]{1,0:T(8,128)(2,1)S(1)}, f32[10,64,128]{2,1,0:T(8,128)S(1)}, f32[10,64,128]{2,1,0:T(8,128)S(1)}) custom-call(bf16[1024,768]{1,0:T(8,128)(2,1)S(1)} %get-tuple-element.37.refs_0_, f32[6,128,128]{2,1,0:T(8,128)S(1)} %bitcast.19, f32[6,128,128]{2,1,0:T(8,128)S(1)} %bitcast.21, bf16[128,768]{1,0:T(8,128)(2,1)S(1)} %solve4.1.refs_3_, ...), custom_call_target="tpu_custom_call" | custom-call | tf_op jit(solution)/shard_map/share5/pallas_call | solution.py:798
  174.3 3.4 %last.1 = bf16[1024,512]{1,0:T(8,128)(2,1)} custom-call(bf16[1024,640]{1,0:T(8,128)(2,1)S(1)} %get-tuple-element.40.columns_ref, f32[5,128,128]{2,1,0:T(8,128)S(1)} %bitcast.22, f32[5,128,128]{2,1,0:T(8,128)S(1)} %bitcast.23), custom_call_target="tpu_custom_call" | custom-call | tf_op jit(solution)/shard_map/last/pallas_call | solution.py:298
Async XLA Ops:
  1.3 1.4 copy-start
  2.7 1.2 copy-start.2
  3.9 0.7 copy-start.3
  4.6 0.7 copy-start.4
  5.3 4.1 %copy-start.1 = (bf16[1024,768]{1,0:T(8,128)(2,1)S(1)}, bf16[1024,768]{1,0:T(8,128)(2,1)}, u32[]{:S(2)}) copy-start(bf16[1024,768]{1,0:T(8,128)(2,1)} %refs_4_.9) | copy-start | bytes 4718596

commit v4 on v3

--- a/solution.py
+++ b/solution.py
@@ -182,21 +182,17 @@
 
 
 def start_kernel(
-    shift_ref, split_ref, terms_ref, order_ref, coupling_ref, higher_ref,
+    rows_ref, coupling_ref, higher_ref,
     columns_ref, own_ref, sums_ref, mix_ref,
     basis_t_ref, inv_ref, pow_ref,
 ):
     rows, levels = coupling_ref.shape
     blocks = rows // RANK
 
-    shift = shift_ref[0]
-    split = split_ref[0]
     for block in range(blocks):
         here = pl.ds(block * RANK, RANK)
-        diagonal = shift + terms_ref[pl.ds(block, 1), :]
-        scale = jnp.broadcast_to(1.0 / diagonal, (RANK, RANK)).T
-        mask = jnp.where(order_ref[pl.ds(block, 1), :] < split, 1.0, 0.0)
-        inside_t = jnp.broadcast_to(mask, (RANK, RANK))
+        scale = jnp.broadcast_to(rows_ref[pl.ds(block, 1), :], (RANK, RANK)).T
+        inside_t = jnp.broadcast_to(rows_ref[pl.ds(blocks + block, 1), :], (RANK, RANK))
         inside = inside_t.T
         for first in range(0, levels, RANK):
             value = coupling_ref[here, pl.ds(first, RANK)].astype(jnp.float32)
@@ -256,7 +252,9 @@
     width = levels + higher.shape[1]
     blocks = rows // RANK
     whole = pl.BlockSpec(memory_space=VMEM)
-    scalar = pl.BlockSpec(memory_space=pltpu.SMEM)
+    scale = 1.0 / (shift[0] + terms)
+    inside = (order < split[0]).astype(jnp.float32)
+    per_row = jnp.concatenate([scale, inside]).reshape(2 * blocks, RANK)
     return pl.pallas_call(
         start_kernel,
         name="start",
@@ -266,7 +264,7 @@
             jax.ShapeDtypeStruct((2 * RANK, width), jnp.float32),
             jax.ShapeDtypeStruct((2 * RANK, 6 * RANK), jnp.bfloat16),
         ),
-        in_specs=[scalar, scalar, whole, whole, whole, whole],
+        in_specs=[whole] * 3,
         out_specs=(whole,) * 4,
         scratch_shapes=[
             VMEM((2 * RANK, rows), jnp.bfloat16),
@@ -274,7 +272,7 @@
             VMEM((RANK, RANK), jnp.float32),
         ],
         compiler_params=pltpu.CompilerParams(vmem_limit_bytes=24 * 2**20),
-    )(shift, split, terms.reshape(blocks, RANK), order.reshape(blocks, RANK), coupling, higher)
+    )(per_row, coupling, higher)
 
 
 def solve_call(level, folded, mine, other):
@@ -310,6 +308,7 @@
     span, kind, pace, prepare, ready, part_ref, mine_ref, other_ref,
     before, after, cross, up_buf, down_buf, half_ref, peer,
     before_sem, after_sem, cross_sem, up_sem, down_sem, pass_sem, swap_sem, trade_sem, peer_sem,
+    skip_sem,
 ):
     chunks = part_ref.shape[0]
     place = lax.axis_index("sub")
@@ -318,6 +317,9 @@
     above = {"sub": lax.rem(place + 1, size)}
     below = {"sub": lax.rem(place + size - 1, size)}
     partner = {"leaf": leaf + 1 - 2 * lax.rem(leaf, 2)}
+    skip = 2 if kind == "core" else 1
+    far_above = {"sub": lax.rem(place + skip, size)}
+    far_below = {"sub": lax.rem(place + size - skip, size)}
     spot = lax.rem(place, span)
     first_child = lax.rem(place // span, 2) == 0
     has_below = spot > 0
@@ -343,8 +345,10 @@
         pl.semaphore_signal(barrier, inc=1, device_id=above)
         if kind == "core":
             pl.semaphore_signal(barrier, inc=1, device_id=partner)
+            pl.semaphore_signal(barrier, inc=1, device_id=far_below)
+            pl.semaphore_signal(barrier, inc=1, device_id=far_above)
         prepare()
-        pl.semaphore_wait(barrier, 3 if kind == "core" else 2)
+        pl.semaphore_wait(barrier, 5 if kind == "core" else 2)
     sum_ref = half_ref if kind == "core" else mine_ref
 
     def copy(src, dst, send, recv, c, to):
@@ -364,6 +368,9 @@
 
     def swap(c, to):
         return copy(sum_ref, cross, swap_sem, cross_sem, c, to)
+
+    def swap_far(c, to):
+        return copy(sum_ref, cross, skip_sem, cross_sem, c, to)
 
     def trade(c):
         return copy(mine_ref, peer, trade_sem, peer_sem, c, partner)
@@ -379,15 +386,15 @@
         reach = span // 2
         upper = spot >= reach
         distance = jnp.where(upper, span - spot, spot + 1)
-        forward_down = upper & (spot > reach)
-        forward_up = jnp.logical_not(upper) & (spot < reach - 1)
+        forward_down = upper & (spot > reach + skip - 1)
+        forward_up = jnp.logical_not(upper) & (spot < reach - skip)
         swap_up = spot == span - 1
         swap_down = spot == 0
     up_from = pace * spot
     down_from = pace * (span - 1 - spot)
     sum_from = jnp.maximum(up_from, down_from)
-    cross_from = pace * (span - 1 + distance)
-    slots = chunks + pace * (span - 1 + reach)
+    cross_from = pace * (span - 1 + (distance + skip - 1) // skip)
+    slots = chunks + pace * (span - 1 + reach // skip)
     if kind == "core":
         slots += pace - 1
 
@@ -461,10 +468,14 @@
             @pl.when(swap_up)
             def _():
                 swap(e, above).start()
+                if skip > 1:
+                    swap_far(e, far_above).start()
 
             @pl.when(swap_down)
             def _():
                 swap(e, below).start()
+                if skip > 1:
+                    swap_far(e, far_below).start()
 
         x = slot - cross_from
 
@@ -475,11 +486,11 @@
 
                 @pl.when(forward_up)
                 def _():
-                    pass_on(x, above).start()
+                    pass_on(x, far_above).start()
 
                 @pl.when(forward_down)
                 def _():
-                    pass_on(x, below).start()
+                    pass_on(x, far_below).start()
 
             if kind == "core":
                 mine_ref[x] = sum_ref[x] + cross[x]
@@ -510,12 +521,14 @@
         @pl.when(swap_up | swap_down)
         def _():
             swap(c, above).wait_send()
+            if skip > 1:
+                swap_far(c, far_above).wait_send()
 
         if reach > 1:
 
             @pl.when(forward_up | forward_down)
             def _():
-                pass_on(c, above).wait_send()
+                pass_on(c, far_above).wait_send()
 
         if kind == "core":
             trade(c).wait_send()
@@ -675,12 +688,23 @@
 
         @pl.when((x == head - 1) & (forward_up | forward_down))
         def _():
-            block = jnp.concatenate([cross[i] for i in range(head)], axis=0)
-            for start in range(head, chunks, head):
-                terms = jnp.concatenate([part_ref[start + i] for i in range(head)], axis=0)
-                product = dot32(block, terms)
-                for i in range(head):
-                    turned[start + i] = product[i * height : (i + 1) * height, :]
+            high, low = halves(jnp.concatenate([cross[i] for i in range(head)], axis=0))
+            block = jnp.concatenate([high, high, low], axis=1)
+            for first in range(head, chunks, 2 * head):
+                starts = range(first, min(first + 2 * head, chunks), head)
+                terms = jnp.concatenate(
+                    [
+                        jnp.concatenate([part_ref[start + i] for i in range(head)], axis=0)
+                        for start in starts
+                    ],
+                    axis=1,
+                )
+                high, low = halves(terms)
+                product = dot16(block, jnp.concatenate([high, low, high], axis=0))
+                for j, start in enumerate(starts):
+                    for i in range(head):
+                        piece = product[i * height : (i + 1) * height, j * RANK : (j + 1) * RANK]
+                        turned[start + i] = piece
 
         u = slot - rise_from
 
@@ -794,7 +818,7 @@
         scratch += [semaphores, semaphores, some, semaphores, semaphores, some, some]
     else:
         share = functools.partial(share_kernel, span, kind, pace)
-        scratch = [buffer] * 7 + [semaphores] * 9
+        scratch = [buffer] * 7 + [semaphores] * 10
     columns, mine, other = pl.pallas_call(
         functools.partial(updates_in, share, level, height, wide),
         name=f"share{level}",

time: 178 us -> 177 us (level)
  the two profiles are of different devices: /device:TPU:109 before, /device:TPU:1 now
where the time goes in v4:
time: 177 us; the launch traced here: 175 us
  Pallas kernels  170 us (96%)
  local copies, waits for them, and re-layouts  2.64 us (1%)
    pallas_call x5, Pallas kernels, share_call(): pl.pallas_call(functools.partial(updates_in, share, level, height, wide),...  157 us
    pallas_call x4, Pallas kernels, solve_call(): pl.pallas_call(functools.partial(solve_kernel, folded), name=f'solve{leve...  4.96 us
    pallas_call x1, Pallas kernels, start_call(): pl.pallas_call(start_kernel, name='start', out_shape=(jax.ShapeDtypeStruc...  3.73 us

profile of v4, /device:TPU:1, one launch (start us, length us, event | category | flops | bytes accessed | tf_op | source)
XLA Modules:
  0.0 174.9 jit_solution(7195851877859601690)
XLA Ops:
  1.3 0.7 divide_bitcast_fusion
  2.0 0.7 compare_convert_fusion
  2.7 0.0 copy-start
  2.7 1.4 copy-done
  4.1 0.0 copy-start.2
  4.1 1.2 copy-done.2
  5.3 0.0 copy-start.1
  5.3 3.7 %start.1 = (bf16[1024,1280]{1,0:T(8,128)(2,1)S(1)}, bf16[1024,256]{1,0:T(8,128)(2,1)S(1)}, f32[256,1280]{1,0:T(8,128)S(1)}, bf16[256,768]{1,0:T(8,128)(2,1)S(1)}) custom-call(f32[16,128]{1,0:T(8,128)S(1)} %pad_maximum_fusion.rows_ref, bf16[1024,768]{1,0:T(8,128)(2,1)S(1)} %copy-done, bf16[1024,512]{1,0:T(8,128)(2,1)S(1)} %copy-done.2), custom_call_target="tpu_custom_call" | custom-call | tf_op jit(solution)/shard_map/start/pallas_call | solution.py:258
  9.1 0.0 copy-done.1
  9.1 12.8 %share1.1 = (bf16[1024,1152]{1,0:T(8,128)(2,1)S(1)}, f32[3,384,128]{2,1,0:T(8,128)S(1)}, f32[3,384,128]{2,1,0:T(8,128)S(1)}) custom-call(bf16[1024,1280]{1,0:T(8,128)(2,1)S(1)} %get-tuple-element.24.refs_0_, bf16[1024,256]{1,0:T(8,128)(2,1)S(1)} %get-tuple-element.25.refs_1_, f32[256,1280]{1,0:T(8,128)S(1)} %get-tuple-element.26.refs_2_, ...), custom_call_target="tpu_custom_call" | custom-call | tf_op jit(solution)/shard_map/share1/pallas_call | solution.py:822
  21.9 1.2 solve1.1.refs_3_
  23.2 27.4 %share2.1 = (bf16[1024,1024]{1,0:T(8,128)(2,1)S(1)}, f32[8,128,128]{2,1,0:T(8,128)S(1)}, f32[8,128,128]{2,1,0:T(8,128)S(1)}) custom-call(bf16[1024,1152]{1,0:T(8,128)(2,1)S(1)} %get-tuple-element.28.refs_0_, f32[9,128,128]{2,1,0:T(8,128)S(1)} %bitcast.16, f32[9,128,128]{2,1,0:T(8,128)S(1)} %bitcast.18, bf16[128,768]{1,0:T(8,128)(2,1)S(1)} %solve1.1.refs_3_, ...), custom_call_target="tpu_custom_call" | custom-call | tf_op jit(solution)/shard_map/share2/pallas_call | solution.py:822
  50.5 1.2 solve2.1.refs_3_
  51.8 33.5 %share3.1 = (bf16[1024,896]{1,0:T(8,128)(2,1)S(1)}, f32[14,64,128]{2,1,0:T(8,128)S(1)}, f32[14,64,128]{2,1,0:T(8,128)S(1)}) custom-call(bf16[1024,1024]{1,0:T(8,128)(2,1)S(1)} %get-tuple-element.31.refs_0_, f32[8,128,128]{2,1,0:T(8,128)S(1)} %get-tuple-element.32.mine_ref.refs_1_, f32[8,128,128]{2,1,0:T(8,128)S(1)} %get-tuple-element.33.other_ref.refs_2_, ...), custom_call_target="tpu_custom_call" | custom-call | tf_op jit(solution)/shard_map/share3/pallas_call | solution.py:822
  85.3 1.2 solve3.1.refs_3_
  86.5 27.9 %share4.1 = (bf16[1024,768]{1,0:T(8,128)(2,1)S(1)}, f32[12,64,128]{2,1,0:T(8,128)S(1)}, f32[12,64,128]{2,1,0:T(8,128)S(1)}) custom-call(bf16[1024,896]{1,0:T(8,128)(2,1)S(1)} %get-tuple-element.34.refs_0_, f32[7,128,128]{2,1,0:T(8,128)S(1)} %bitcast.20, f32[7,128,128]{2,1,0:T(8,128)S(1)} %bitcast.22, bf16[128,768]{1,0:T(8,128)(2,1)S(1)} %solve3.1.refs_3_, ...), custom_call_target="tpu_custom_call" | custom-call | tf_op jit(solution)/shard_map/share4/pallas_call | solution.py:822
  114.4 1.2 solve4.1.refs_3_
  115.7 55.8 %share5.1 = (bf16[1024,640]{1,0:T(8,128)(2,1)S(1)}, f32[10,64,128]{2,1,0:T(8,128)S(1)}, f32[10,64,128]{2,1,0:T(8,128)S(1)}) custom-call(bf16[1024,768]{1,0:T(8,128)(2,1)S(1)} %get-tuple-element.37.refs_0_, f32[6,128,128]{2,1,0:T(8,128)S(1)} %bitcast.24, f32[6,128,128]{2,1,0:T(8,128)S(1)} %bitcast.26, bf16[128,768]{1,0:T(8,128)(2,1)S(1)} %solve4.1.refs_3_, ...), custom_call_target="tpu_custom_call" | custom-call | tf_op jit(solution)/shard_map/share5/pallas_call | solution.py:822
  171.5 3.4 %last.1 = bf16[1024,512]{1,0:T(8,128)(2,1)} custom-call(bf16[1024,640]{1,0:T(8,128)(2,1)S(1)} %get-tuple-element.40.columns_ref, f32[5,128,128]{2,1,0:T(8,128)S(1)} %bitcast.27, f32[5,128,128]{2,1,0:T(8,128)S(1)} %bitcast.28), custom_call_target="tpu_custom_call" | custom-call | tf_op jit(solution)/shard_map/last/pallas_call | solution.py:296
  (1 shorter events, 0.0 us)
Async XLA Ops:
  2.7 1.4 copy-start
  4.1 1.2 copy-start.2
  5.3 3.7 %copy-start.1 = (bf16[1024,768]{1,0:T(8,128)(2,1)S(1)}, bf16[1024,768]{1,0:T(8,128)(2,1)}, u32[]{:S(2)}) copy-start(bf16[1024,768]{1,0:T(8,128)(2,1)} %refs_4_.9) | copy-start | bytes 4718596
